TPU v7x, 32 devices: a whole 2x2x4 slice. The times are simulated.
32 devices in a mesh: src: 4 (over x, core), gy: 4 (over z), gx: 2 (over y).
Axes of the slice: x: 2, y: 2, z: 4, core: 2. Of those that a mesh axis runs over, the one named last changes fastest.
Arguments:
- fields: bfloat16 [5, 256, 256, 1024], P(None, 'src', 'gy', 'gx'), may hold values from -6 to 6
- dx_op: bfloat16 [1024, 1024], P(('gy', 'gx'))
- y_ops: bfloat16 [2, 256, 256], replicated
- dz_op: bfloat16 [256, 256], replicated
- metric_x: float32 [1024], P('gx'), may hold values from 0.5 to 2
- metric_y: float32 [256], P('gy'), may hold values from 0.5 to 2
- metric_z: float32 [256], P('src'), may hold values from 0.5 to 2
- mean_u: float32 [256, 256], P('src', 'gy'), may hold values from 0.2 to 1.5
- surface_rows: bfloat16 [256, 5, 256], P(('src', 'gy', 'gx')), may hold values from -6 to 6
- row_block: int32 [256], P(('src', 'gy', 'gx')), may hold values from 0 to 8191
- row_offsets: int32 [32, 9], P(('src', 'gy', 'gx')), may hold values from 0 to 8, as said below
Outputs:
- fields_next: bfloat16 [5, 256, 256, 1024], P(None, 'src', 'gy', 'gx')
Inputs may be any that keep to these rules, and one draw needn't show every extreme that they name: row_offsets[d, 0] = 0 and row_offsets[d, 8] = 8; the offsets never fall; at most 2 rows of one device go to one destination, and in every draw some destination receives 2 rows from every device of its src index.
All inputs are finite; a program needn't handle non-finite values.
Results may differ from a plain program's by a relative error of at most 0.0049.
Values may be sent and summed in bfloat16 or wider, within the bound.
No kernel may reach another device: no remote copies, remote signals or barrier semaphores. Data moves between devices by JAX's collectives and lax.ppermute only.
A program may use at most 384 MiB of HBM per device.

v0:
```python
import jax
import jax.numpy as jnp
from jax import lax
from jax.experimental import pallas as pl
from jax.experimental.pallas import tpu as pltpu
from jax.sharding import PartitionSpec as P


ROW_LEN = 256
CAP = 2
DIGIT = 128
SLAB = 16
STEP_SIZE = 0.25
Y_ITEMS = (
    ("in", 2),
    ("in", 0),
    ("in", 4),
    ("in", 1),
    ("out", 0),
    ("in", 3),
    ("out", 2),
    ("out", 4),
    ("out", 1),
    ("out", 3),
)
IN_FLIGHT = 3
AFTER_REST = 1
AFTER_FIRST = 3
Y_TERM = {0: 2, 2: 4, 4: 2}


class Axis:
    def __init__(self, name):
        self.name = name
        self.size = lax.axis_size(name)
        self.me = lax.axis_index(name)
        self.xor = self.size & (self.size - 1) == 0

    def dest(self, k):
        return jnp.bitwise_xor(self.me, k) if self.xor else (self.me + k) % self.size

    def source(self, k):
        return jnp.bitwise_xor(self.me, k) if self.xor else (self.me - k) % self.size

    def send(self, array, k):
        pairs = [(i, i ^ k if self.xor else (i + k) % self.size) for i in range(self.size)]
        return lax.ppermute(array, self.name, pairs)

    def gather(self, array):
        return [array] + [self.send(array, k) for k in range(1, self.size)]

    def steps(self):
        return jnp.arange(self.size, dtype=jnp.int32)

    def in_place_order(self, pieces):
        return jnp.take(jnp.stack(pieces), self.source(self.steps()), axis=0)


def cost(flops, bytes_accessed):
    return pl.CostEstimate(flops=int(flops), transcendentals=0, bytes_accessed=int(bytes_accessed))


def largest_divisor(extent, most):
    return max(d for d in range(1, min(extent, most) + 1) if extent % d == 0)


def y_part(fields, place, variable, arrived, term, term_arrived, matrices, scale):
    num = len(arrived) + 1
    planes, rows, cells = arrived[0].shape
    zb = largest_divisor(planes, 4)
    per = planes // zb
    extent = num * rows
    full = jax.ShapeDtypeStruct(arrived[0].shape, jnp.bfloat16)
    groups = [(variable, arrived)] + ([] if term is None else [(term, term_arrived)])
    total = num * len(groups)

    def kernel(place_ref, *refs):
        mats_ref, scale_ref = refs[total : total + 2]
        out_refs = refs[total + 2 :]

        def product(group, matrix, z):
            first, *others = refs[group * num : (group + 1) * num]
            lines = jnp.concatenate([first[0, z]] + [r[z] for r in others], axis=0)
            return jnp.dot(mats_ref[matrix], lines, preferred_element_type=jnp.float32)

        for z in range(zb):
            acc = product(0, 1, z)
            if term is not None:
                acc += scale_ref[...] * product(1, 0, z)
            for k in range(num):
                out_refs[k][z] = acc[k * rows : (k + 1) * rows].astype(jnp.bfloat16)

    def own_place(v):
        return lambda i, p: (v, p[0] * per + i, 0, 0)

    block = pl.BlockSpec((zb, rows, cells), lambda i, p: (i, 0, 0))
    in_specs = []
    operands = []
    for v, blocks in groups:
        in_specs += [pl.BlockSpec((1, zb, rows, cells), own_place(v))] + [block] * (num - 1)
        operands += [fields] + list(blocks)
    in_specs += [
        pl.BlockSpec((2, extent, extent), lambda i, p: (0, 0, 0)),
        pl.BlockSpec((extent, 1), lambda i, p: (0, 0)),
    ]
    return pl.pallas_call(
        kernel,
        grid_spec=pltpu.PrefetchScalarGridSpec(
            num_scalar_prefetch=1, grid=(per,), in_specs=in_specs, out_specs=[block] * num
        ),
        out_shape=[full] * num,
        cost_estimate=cost(
            2 * extent * extent * planes * cells * len(groups),
            2 * extent * planes * cells * (len(groups) + 1),
        ),
    )(place, *operands, matrices, scale)


def z_part(fields, arrived, operator, scale):
    _, planes, rows, cells = fields.shape
    num = len(arrived) + 1
    slab = largest_divisor(rows, SLAB)
    size = planes * slab

    def kernel(own_ref, *refs):
        in_refs = (own_ref,) + refs[: num - 1]
        op_ref, scale_ref, out_ref = refs[num - 1 :]
        acc = jnp.zeros((size, cells), jnp.float32)
        for k in range(num):
            acc += jnp.dot(op_ref[k], in_refs[k][0].reshape(size, cells), preferred_element_type=jnp.float32)
        out_ref[0] = (scale_ref[...] * acc).reshape(planes, slab, cells).astype(jnp.bfloat16)

    block = (1, planes, slab, cells)
    here = pl.BlockSpec(block, lambda a, i: (a, 0, i, 0))
    return pl.pallas_call(
        kernel,
        grid=(2, rows // slab),
        in_specs=[pl.BlockSpec(block, lambda a, i: (a + 3, 0, i, 0))]
        + [here] * (num - 1)
        + [
            pl.BlockSpec((num, size, size), lambda a, i: (0, 0, 0)),
            pl.BlockSpec((size, 1), lambda a, i: (0, 0)),
        ],
        out_specs=here,
        out_shape=jax.ShapeDtypeStruct((2, planes, rows, cells), jnp.bfloat16),
        name="z_part",
        cost_estimate=cost(
            4 * num * size * size * cells * (rows // slab), 4 * (num + 1) * planes * rows * cells
        ),
    )(fields, *arrived, operator, scale)


def x_part(fields, arrived, operator, scale_x, speed, z_terms, rows_in, targets):
    num_vars, planes, rows, cells = fields.shape
    num = len(arrived) + 1
    zb = largest_divisor(planes, max(1, 256 // rows))
    size = zb * rows
    num_rows = targets.shape[0]
    width = min(ROW_LEN, cells)

    def kernel(targets_ref, own_ref, *refs):
        in_refs = (own_ref,) + refs[: num - 1]
        op_ref, scale_ref, speed_ref, z_ref, rows_ref, out_ref = refs[num - 1 :]
        speed_col = speed_ref[...].reshape(size, 1)

        def slope(v):
            acc = jnp.dot(
                in_refs[0][v].reshape(size, cells), op_ref[0], preferred_element_type=jnp.float32
            )
            for k in range(1, num):
                acc += jnp.dot(
                    in_refs[k][v].reshape(size, cells), op_ref[k], preferred_element_type=jnp.float32
                )
            return acc * scale_ref[...]

        def z_term(a):
            return z_ref[a].reshape(size, cells).astype(jnp.float32)

        def put(v, value):
            out_ref[v] = (-STEP_SIZE * value).reshape(zb, rows, cells)

        slope_u = slope(1)
        slope_p = slope(4)
        divergence = slope_u + z_term(0)
        put(1, speed_col * slope_u + slope_p)
        put(4, speed_col * slope_p + divergence)
        put(0, speed_col * slope(0) + divergence)
        put(2, speed_col * slope(2))
        put(3, speed_col * slope(3) + z_term(1))
        first = pl.program_id(0) * zb

        @pl.loop(0, num_rows)
        def _(r):
            for piece in range(ROW_LEN // width):
                cell = targets_ref[r] * ROW_LEN + piece * width
                plane = cell // (rows * cells) - first

                @pl.when((plane >= 0) & (plane < zb))
                def _():
                    row = (cell // cells) % rows
                    start = pl.multiple_of(cell % cells, width)
                    for v in range(num_vars):
                        place = (v, plane, pl.ds(row, 1), pl.ds(start, width))
                        out_ref[place] += rows_ref[r, v : v + 1, piece * width : (piece + 1) * width]

    block = pl.BlockSpec((num_vars, zb, rows, cells), lambda i, t: (0, i, 0, 0))
    return pl.pallas_call(
        kernel,
        grid_spec=pltpu.PrefetchScalarGridSpec(
            num_scalar_prefetch=1,
            grid=(planes // zb,),
            in_specs=[block] * num
            + [
                pl.BlockSpec((num, cells, cells), lambda i, t: (0, 0, 0)),
                pl.BlockSpec((1, cells), lambda i, t: (0, 0)),
                pl.BlockSpec((zb, rows, 1), lambda i, t: (i, 0, 0)),
                pl.BlockSpec((2, zb, rows, cells), lambda i, t: (0, i, 0, 0)),
                pl.BlockSpec(rows_in.shape, lambda i, t: (0, 0, 0)),
            ],
            out_specs=block,
        ),
        out_shape=jax.ShapeDtypeStruct(fields.shape, jnp.float32),
        name="x_part",
        cost_estimate=cost(
            2 * num_vars * planes * rows * cells * cells * num,
            num_vars * planes * rows * cells * (2 * num + 5),
        ),
    )(targets, fields, *arrived, operator, scale_x, speed, z_terms, rows_in)


def finish(total, rest, part, variable, place):
    planes, rows, cells = part.shape
    zb = largest_divisor(planes, 8)
    per = planes // zb

    def kernel(place_ref, rest_ref, part_ref, *refs):
        refs[-1][0] = (rest_ref[0] + part_ref[...].astype(jnp.float32)).astype(jnp.bfloat16)

    big = pl.BlockSpec((1, zb, rows, cells), lambda i, p: (variable, p[0] * per + i, 0, 0))
    in_specs = [big, pl.BlockSpec((zb, rows, cells), lambda i, p: (i, 0, 0))]
    operands = [rest, part]
    aliases = {}
    if total is not None:
        in_specs.append(pl.BlockSpec(memory_space=pl.ANY))
        operands.append(total)
        aliases = {3: 0}
    return pl.pallas_call(
        kernel,
        grid_spec=pltpu.PrefetchScalarGridSpec(
            num_scalar_prefetch=1, grid=(per,), in_specs=in_specs, out_specs=big
        ),
        out_shape=jax.ShapeDtypeStruct(rest.shape, jnp.bfloat16),
        input_output_aliases=aliases,
        cost_estimate=cost(planes * rows * cells, 8 * planes * rows * cells),
    )(place, *operands)


def route_rows(gy, gx, surface_rows, row_block, row_offsets, num_blocks):
    num_vars = surface_rows.shape[1]
    starts = row_offsets[0, :-1]
    counts = row_offsets[0, 1:] - starts
    slots = jnp.arange(CAP, dtype=jnp.int32)
    is_valid = slots[None, :] < counts[:, None]
    row_index = jnp.where(is_valid, starts[:, None] + slots[None, :], 0).reshape(-1)
    valid = is_valid.reshape(-1)[:, None]
    picked = jnp.take(surface_rows.reshape(-1, num_vars * ROW_LEN), row_index, axis=0)
    picked = jnp.where(valid, picked, jnp.zeros((), jnp.bfloat16))
    blocks = jnp.where(is_valid.reshape(-1), jnp.take(row_block, row_index), 0)
    digits = []
    scale = 1
    while scale < num_blocks:
        digits.append((blocks // scale) % DIGIT)
        scale *= DIGIT
    tail = jnp.stack(digits, axis=1).astype(jnp.bfloat16)
    tail = jnp.pad(tail, ((0, 0), (0, -len(digits) % 128)))
    packed = jnp.concatenate([picked, tail], axis=1).reshape(gy.size, gx.size, CAP, -1)
    for axis in (gy, gx):
        by_dest = [lax.dynamic_index_in_dim(packed, axis.dest(k), 0, keepdims=False) for k in range(axis.size)]
        got = [by_dest[0]] + [axis.send(by_dest[k], k) for k in range(1, axis.size)]
        packed = jnp.stack(got, axis=1) if axis is gy else jnp.stack(got)
    flat = packed.reshape(-1, packed.shape[-1])
    rows_in = flat[:, : num_vars * ROW_LEN].astype(jnp.float32).reshape(-1, num_vars, ROW_LEN)
    targets = jnp.zeros((flat.shape[0],), jnp.int32)
    for place in range(len(digits)):
        digit = flat[:, num_vars * ROW_LEN + place].astype(jnp.float32).astype(jnp.int32)
        targets += digit * DIGIT**place
    return rows_in, targets


def x_operator(src, gy, gx, dx_op):
    rows, extent = dx_op.shape
    cells = rows * gy.size
    share = rows // src.size if rows % src.size == 0 else rows
    split = share != rows
    piece = lax.dynamic_slice_in_dim(dx_op, src.me * share, share, 0) if split else dx_op
    columns = gy.in_place_order(gy.gather(piece))
    blocks = gx.in_place_order(gx.gather(columns)).swapaxes(0, 1)
    blocks = blocks.reshape(gy.size * gx.size, share, extent)
    needed = lax.dynamic_slice_in_dim(blocks, gx.me * gy.size, gy.size, 0)
    if split:
        needed = src.in_place_order(src.gather(needed)).swapaxes(0, 1)
    turned = needed.reshape(cells, extent).T.reshape(gx.size, cells, cells)
    return jnp.take(turned, gx.source(gx.steps()), axis=0)


def z_operator(src, dz_op, planes, slab):
    own = lax.dynamic_slice_in_dim(dz_op, src.me * planes, planes, 0)
    blocks = own.reshape(planes, src.size, planes).swapaxes(0, 1)
    blocks = jnp.take(blocks, src.source(src.steps()), axis=0)
    size = planes * slab
    index = jnp.arange(size, dtype=jnp.int32)
    spread = (index[:, None] // slab == jnp.arange(planes, dtype=jnp.int32)[None, :]).astype(jnp.bfloat16)
    same_row = (index[:, None] % slab) == (index[None, :] % slab)
    wide = jnp.einsum("pi,kij->kpj", spread, blocks, preferred_element_type=jnp.float32).astype(jnp.bfloat16)
    wide = jnp.einsum("kpj,qj->kpq", wide, spread, preferred_element_type=jnp.float32).astype(jnp.bfloat16)
    return jnp.where(same_row[None], wide, jnp.zeros((), jnp.bfloat16))


def y_operator(gy, y_ops, rows):
    num = y_ops.shape[0]
    blocks = y_ops.reshape(num, gy.size, rows, gy.size, rows)
    blocks = jnp.take(blocks, gy.dest(gy.steps()), axis=1)
    blocks = jnp.take(blocks, gy.source(gy.steps()), axis=3)
    return blocks.reshape(y_ops.shape)


def on_device(
    fields,
    dx_op,
    y_ops,
    dz_op,
    metric_x,
    metric_y,
    metric_z,
    mean_u,
    surface_rows,
    row_block,
    row_offsets,
):
    _, planes, rows, cells = fields.shape
    src, gy, gx = Axis("src"), Axis("gy"), Axis("gx")
    share = planes // gy.size

    after = lax.optimization_barrier
    place = gy.me.reshape(1).astype(jnp.int32)

    def z_block(array, v, k):
        return lax.dynamic_slice(array, (v, gy.dest(k) * share, 0, 0), (1, share, rows, cells))[0]

    matrices = y_operator(gy, y_ops, rows)
    metric_all = gy.in_place_order(gy.gather(metric_y.reshape(1, rows)))
    scale_y = -STEP_SIZE * jnp.take(metric_all, gy.dest(gy.steps()), axis=0).reshape(-1, 1)
    slab = largest_divisor(rows, SLAB)
    z_scale = jnp.repeat(metric_z, slab).reshape(-1, 1)
    num_blocks = planes * rows * cells // ROW_LEN
    rows_in, targets = route_rows(gy, gx, surface_rows, row_block, row_offsets, num_blocks)
    turned = x_operator(src, gy, gx, dx_op)

    x_fields, *_ = after((fields, turned, rows_in))
    x_arrived = [gx.send(x_fields, k) for k in range(1, gx.size)]
    z_fields, _ = after((fields, turned))
    z_arrived = [src.send(z_fields[3:5], k) for k in range(1, src.size)]
    z_terms = z_part(fields, z_arrived, z_operator(src, dz_op, planes, slab), z_scale)
    rest = x_part(
        fields,
        x_arrived,
        turned,
        metric_x.reshape(1, cells),
        mean_u.reshape(planes, rows, 1),
        z_terms,
        rows_in,
        targets,
    )

    def finish_variable(total, v):
        for k in range(gy.size):
            at = gy.source(k).reshape(1).astype(jnp.int32)
            total = finish(total, rest, parts[v][k], v, at)
        return total

    held, parts, done = {}, {}, []
    total = None
    finished = []
    blocks = None
    for kind, v in Y_ITEMS:
        behind = done[-IN_FLIGHT] if len(done) >= IN_FLIGHT else None
        if kind == "in":
            source = fields
            if behind is not None or blocks is not None:
                source, _ = after((fields, blocks if behind is None else behind))
            blocks = {}
            for k in step_order(gy.size):
                blocks[k] = z_block(source, v, k)
                if not done and len(blocks) == 1:
                    source, blocks[k] = after((source, blocks[k]))
            result = held[v] = {k: gy.send(blocks[k], k) for k in blocks}
        else:
            term = Y_TERM.get(v)
            lines = [held[v][k] for k in range(1, gy.size)]
            term_lines = [] if term is None else [held[term][k] for k in range(1, gy.size)]
            whole = y_part(fields, place, v, lines, term, term_lines, matrices, scale_y)
            going = {k: whole[k] for k in step_order(gy.size)}
            if behind is not None:
                going, _ = after((going, behind))
            if v == AFTER_REST:
                going, rest = after((going, rest))
            if v == AFTER_FIRST:
                finished = [Y_ITEMS[4][1]]
                total = finish_variable(total, finished[0])
                going, total = after((going, total))
            result = {k: gy.send(going[k], k) for k in going}
            parts[v] = [whole[0]] + [result[k] for k in range(1, gy.size)]
        done.append(result)
    for kind, v in Y_ITEMS:
        if kind == "out" and v not in finished:
            total = finish_variable(total, v)
    return total


def step_order(size):
    half = size // 2
    return list(range(half, size)) + list(range(1, half))


def solution(mesh):
    return jax.shard_map(
        on_device,
        mesh=mesh,
        in_specs=(
            P(None, "src", "gy", "gx"),
            P(("gy", "gx"), None),
            P(),
            P(),
            P("gx"),
            P("gy"),
            P("src"),
            P("src", "gy"),
            P(("src", "gy", "gx"), None, None),
            P(("src", "gy", "gx")),
            P(("src", "gy", "gx"), None),
        ),
        out_specs=P(None, "src", "gy", "gx"),
        check_vma=False,
    )
```

profile of v0, /device:TPU:0, one launch (start us, length us, event | category | flops | bytes accessed | tf_op | source)
XLA Modules:
  0.0 1028.2 jit_solution(113083422445641336)
XLA Ops:
  1.0 4.1 collective-permute-start.20
  19.4 3.9 collective-permute-done.21
  25.9 4.6 collective-permute-done.22
  34.2 5.4 collective-permute-done.24
  39.6 2.7 collective-permute-done.25
  51.7 3.2 collective-permute-start
  55.9 63.1 %collective-permute-done.8 = f32[1,64]{1,0:T(1,128)S(1)} collective-permute-done((f32[1,64]{1,0:T(1,128)S(1)}, f32[1,64]{1,0:T(1,128)S(1)}, u32[]{:S(2)}, u32[]{:S(2)}) %collective-permute-start.8) | collective-permute-done | bytes 288 | tf_op jit(solution)/shard_map/ppermute | solution.py:47
  119.0 24.3 %collective-permute-start.7 = (f32[1,64]{1,0:T(1,128)S(1)}, f32[1,64]{1,0:T(1,128)S(1)}, u32[]{:S(2)}, u32[]{:S(2)}) collective-permute-start(f32[1,64]{1,0:T(1,128)S(1)} %bitcast.154), channel_id=1, source_target_pairs={{0,4},{2,6},{4,0},{6,2},{1,5},{3,7},{5,1},{7,3},{8,12},{10,14},{12... | collective-permute-start | bytes 776 | tf_op jit(solution)/shard_map/ppermute | solution.py:47
  148.6 2.7 collective-permute-start.35
  153.1 3.5 dynamic-slice_bitcast_fusion.3
  156.6 2.6 collective-permute-start.11
  159.2 3.2 dynamic-slice_bitcast_fusion.9
  162.4 14.3 %collective-permute-done.35.refs_3_ = bf16[16,64,512]{2,1,0:T(8,128)(2,1)} collective-permute-done((bf16[16,64,512]{2,1,0:T(8,128)(2,1)S(1)}, bf16[16,64,512]{2,1,0:T(8,128)(2,1)}, u32[]{:S(2)}, u32[]{:S(2)}) %collective-permute-start.35) | collective-permute-done | bytes 1048608 | tf_op jit(solution)/shard_map/ppermute | solution.py:47
  176.7 46.6 %collective-permute-start.10 = (bf16[16,64,512]{2,1,0:T(8,128)(2,1)}, bf16[16,64,512]{2,1,0:T(8,128)(2,1)}, u32[]{:S(2)}, u32[]{:S(2)}) collective-permute-start(bf16[16,64,512]{2,1,0:T(8,128)(2,1)} %get-tuple-element.114), channel_id=1, source_target_pairs={{0,4},{2,6},{4,0},{6,2},{1,5},{3,7},{5,1},{7,3},{8,12},{10,14},{12... | collective-permute-start | bytes 3145736 | tf_op jit(solution)/shard_map/ppermute | solution.py:47
  223.4 63.4 %collective-permute-done.34.refs_2_ = bf16[16,64,512]{2,1,0:T(8,128)(2,1)} collective-permute-done((bf16[16,64,512]{2,1,0:T(8,128)(2,1)S(1)}, bf16[16,64,512]{2,1,0:T(8,128)(2,1)}, u32[]{:S(2)}, u32[]{:S(2)}) %collective-permute-start.34) | collective-permute-done | bytes 1048608 | tf_op jit(solution)/shard_map/ppermute | solution.py:47
  289.0 55.3 %collective-permute-start.4 = (bf16[16,64,512]{2,1,0:T(8,128)(2,1)S(1)}, bf16[16,64,512]{2,1,0:T(8,128)(2,1)}, u32[]{:S(2)}, u32[]{:S(2)}) collective-permute-start(bf16[16,64,512]{2,1,0:T(8,128)(2,1)S(1)} %get-tuple-element.120), channel_id=1, source_target_pairs={{0,4},{2,6},{4,0},{6,2},{1,5},{3,7},{5,1},{7,3},{8,12},{10,14},{12... | collective-permute-start | bytes 3145736 | tf_op jit(solution)/shard_map/ppermute | solution.py:47
  344.3 7.9 slice.25
  352.2 24.4 %collective-permute-done.10.refs_6_.refs_2_ = bf16[16,64,512]{2,1,0:T(8,128)(2,1)} collective-permute-done((bf16[16,64,512]{2,1,0:T(8,128)(2,1)}, bf16[16,64,512]{2,1,0:T(8,128)(2,1)}, u32[]{:S(2)}, u32[]{:S(2)}) %collective-permute-start.10) | collective-permute-done | bytes 1048608 | tf_op jit(solution)/shard_map/ppermute | solution.py:47
  378.5 41.5 %collective-permute-done.4.refs_2_ = bf16[16,64,512]{2,1,0:T(8,128)(2,1)} collective-permute-done((bf16[16,64,512]{2,1,0:T(8,128)(2,1)S(1)}, bf16[16,64,512]{2,1,0:T(8,128)(2,1)}, u32[]{:S(2)}, u32[]{:S(2)}) %collective-permute-start.4) | collective-permute-done | bytes 1048608 | tf_op jit(solution)/shard_map/ppermute | solution.py:47
  420.1 3.5 dynamic-slice_bitcast_fusion
  423.6 20.1 %collective-permute-done.3.refs_1_ = bf16[16,64,512]{2,1,0:T(8,128)(2,1)S(1)} collective-permute-done((bf16[16,64,512]{2,1,0:T(8,128)(2,1)S(1)}, bf16[16,64,512]{2,1,0:T(8,128)(2,1)S(1)}, u32[]{:S(2)}, u32[]{:S(2)}) %collective-permute-start.3) | collective-permute-done | bytes 1048608 | tf_op jit(solution)/shard_map/ppermute | solution.py:47
  446.0 22.5 %collective-permute-done.14.refs_3_ = bf16[16,64,512]{2,1,0:T(8,128)(2,1)S(1)} collective-permute-done((bf16[16,64,512]{2,1,0:T(8,128)(2,1)S(1)}, bf16[16,64,512]{2,1,0:T(8,128)(2,1)S(1)}, u32[]{:S(2)}, u32[]{:S(2)}) %collective-permute-start.14) | collective-permute-done | bytes 1048608 | tf_op jit(solution)/shard_map/ppermute | solution.py:47
  469.5 21.9 %collective-permute-start.13 = (bf16[16,64,512]{2,1,0:T(8,128)(2,1)}, bf16[16,64,512]{2,1,0:T(8,128)(2,1)}, u32[]{:S(2)}, u32[]{:S(2)}) collective-permute-start(bf16[16,64,512]{2,1,0:T(8,128)(2,1)} %get-tuple-element.111), channel_id=1, source_target_pairs={{0,4},{2,6},{4,0},{6,2},{1,5},{3,7},{5,1},{7,3},{8,12},{10,14},{12... | collective-permute-start | bytes 3145736 | tf_op jit(solution)/shard_map/ppermute | solution.py:47
  498.9 37.0 %collective-permute-done.13.refs_2_ = bf16[16,64,512]{2,1,0:T(8,128)(2,1)} collective-permute-done((bf16[16,64,512]{2,1,0:T(8,128)(2,1)}, bf16[16,64,512]{2,1,0:T(8,128)(2,1)}, u32[]{:S(2)}, u32[]{:S(2)}) %collective-permute-start.13) | collective-permute-done | bytes 1048608 | tf_op jit(solution)/shard_map/ppermute | solution.py:47
  547.0 7.3 shard_map.112
  554.2 5.8 collective-permute-done.12.refs_1_
  560.9 24.3 %collective-permute-done.36.part_ref = bf16[16,64,512]{2,1,0:T(8,128)(2,1)} collective-permute-done((bf16[16,64,512]{2,1,0:T(8,128)(2,1)}, bf16[16,64,512]{2,1,0:T(8,128)(2,1)}, u32[]{:S(2)}, u32[]{:S(2)}) %collective-permute-start.36) | collective-permute-done | bytes 1048608 | tf_op jit(solution)/shard_map/ppermute | solution.py:47
  585.2 20.9 %collective-permute-start.37 = (bf16[16,64,512]{2,1,0:T(8,128)(2,1)}, bf16[16,64,512]{2,1,0:T(8,128)(2,1)S(1)}, u32[]{:S(2)}, u32[]{:S(2)}) collective-permute-start(bf16[16,64,512]{2,1,0:T(8,128)(2,1)} %get-tuple-element.88), channel_id=1, source_target_pairs={{0,4},{2,6},{4,0},{6,2},{1,5},{3,7},{5,1},{7,3},{8,12},{10,14},{12... | collective-permute-start | bytes 3145736 | tf_op jit(solution)/shard_map/ppermute | solution.py:47
  608.2 43.0 %collective-permute-done.37.part_ref = bf16[16,64,512]{2,1,0:T(8,128)(2,1)S(1)} collective-permute-done((bf16[16,64,512]{2,1,0:T(8,128)(2,1)}, bf16[16,64,512]{2,1,0:T(8,128)(2,1)S(1)}, u32[]{:S(2)}, u32[]{:S(2)}) %collective-permute-start.37) | collective-permute-done | bytes 1048608 | tf_op jit(solution)/shard_map/ppermute | solution.py:47
  651.2 5.2 convert_select_fusion.refs_3_
  660.4 7.2 shard_map.117
  667.6 7.2 shard_map.111
  674.9 5.6 shard_map.109
  684.1 54.3 %collective-permute-done.28.refs_1_ = bf16[2,64,64,512]{3,2,1,0:T(8,128)(2,1)} collective-permute-done((bf16[2,64,64,512]{3,2,1,0:T(8,128)(2,1)}, bf16[2,64,64,512]{3,2,1,0:T(8,128)(2,1)}, u32[]{:S(2)}, u32[]{:S(2)}) %collective-permute-start.28) | collective-permute-done | bytes 8388640 | tf_op jit(solution)/shard_map/ppermute | solution.py:47
  738.8 3.4 collective-permute-start.31
  742.2 42.2 %z_part.1.refs_4_ = bf16[2,64,64,512]{3,2,1,0:T(8,128)(2,1)} custom-call(bf16[5,64,64,512]{3,2,1,0:T(8,128)(2,1)} %refs_4_.5, bf16[2,64,64,512]{3,2,1,0:T(8,128)(2,1)} %collective-permute-done.27.refs_0_, bf16[2,64,64,512]{3,2,1,0:T(8,128)(2,1)} %collective-permute-done.28.refs_1_, bf16[2,64,64,512]{3,2,1,0:T(8,128)(2,1)} %collective-permute-done.29.refs_2_, ...), custom_call_target="tpu_custom_call" | custom-call | flops 34359738368 | bytes 41943040 | tf_op jit(solution)/shard_map/z_part/pallas_call | solution.py:135
  785.0 42.8 %x_part.1.rest_ref = f32[5,64,64,512]{3,2,1,0:T(8,128)} custom-call(s32[16]{0:T(128)} %add_bitcast_fusion.targets_ref, bf16[5,64,64,512]{3,2,1,0:T(8,128)(2,1)} %refs_4_.5, bf16[5,64,64,512]{3,2,1,0:T(8,128)(2,1)} %collective-permute-done.26.refs_0_, bf16[2,512,512]{2,1,0:T(8,128)(2,1)} %broadcast_select_fusion.refs_1_, f32[1,512]{1,0:T(1,128)} %bitcast.152, ...), custom_call_target="tpu_custom_call" | custom-call | flops 21474836480 | bytes 94371840 | tf_op jit(solution)/shard_map/x_part/pallas_call | solution.py:207
  828.1 13.1 %collective-permute-done.31.part_ref = bf16[16,64,512]{2,1,0:T(8,128)(2,1)S(1)} collective-permute-done((bf16[16,64,512]{2,1,0:T(8,128)(2,1)}, bf16[16,64,512]{2,1,0:T(8,128)(2,1)S(1)}, u32[]{:S(2)}, u32[]{:S(2)}) %collective-permute-start.31) | collective-permute-done | bytes 1048608 | tf_op jit(solution)/shard_map/ppermute | solution.py:47
  841.2 6.0 shard_map.110
  847.2 16.3 %collective-permute-start.43 = (bf16[16,64,512]{2,1,0:T(8,128)(2,1)}, bf16[16,64,512]{2,1,0:T(8,128)(2,1)}, u32[]{:S(2)}, u32[]{:S(2)}) collective-permute-start(bf16[16,64,512]{2,1,0:T(8,128)(2,1)} %get-tuple-element.96), channel_id=1, source_target_pairs={{0,4},{2,6},{4,0},{6,2},{1,5},{3,7},{5,1},{7,3},{8,12},{10,14},{12... | collective-permute-start | bytes 3145736 | tf_op jit(solution)/shard_map/ppermute | solution.py:47
  863.5 2.7 shard_map.113.refs_0_
  866.2 2.7 shard_map.114.refs_0_
  868.9 2.7 shard_map.115.refs_0_
  871.7 2.7 shard_map.116.refs_0_
  878.8 19.7 %collective-permute-done.44.part_ref = bf16[16,64,512]{2,1,0:T(8,128)(2,1)} collective-permute-done((bf16[16,64,512]{2,1,0:T(8,128)(2,1)}, bf16[16,64,512]{2,1,0:T(8,128)(2,1)}, u32[]{:S(2)}, u32[]{:S(2)}) %collective-permute-start.44) | collective-permute-done | bytes 1048608 | tf_op jit(solution)/shard_map/ppermute | solution.py:47
  898.4 2.7 shard_map.118.refs_0_
  901.2 2.7 shard_map.119.refs_0_
  903.9 2.7 shard_map.120.refs_0_
  906.6 2.7 shard_map.121.refs_0_
  909.3 2.7 shard_map.122.refs_0_
  912.0 2.7 shard_map.123.refs_0_
  914.7 2.7 shard_map.124.refs_0_
  917.4 2.7 shard_map.125.refs_0_
  920.2 2.7 shard_map.126.refs_0_
  922.9 2.7 shard_map.127.refs_0_
  925.6 7.2 collective-permute-done.43.part_ref
  932.8 2.7 shard_map.128.refs_0_
  935.5 2.7 shard_map.129.refs_0_
  938.2 2.7 shard_map.130.refs_0_
  941.0 12.0 %collective-permute-done.41.part_ref = bf16[16,64,512]{2,1,0:T(8,128)(2,1)} collective-permute-done((bf16[16,64,512]{2,1,0:T(8,128)(2,1)}, bf16[16,64,512]{2,1,0:T(8,128)(2,1)}, u32[]{:S(2)}, u32[]{:S(2)}) %collective-permute-start.41) | collective-permute-done | bytes 1048608 | tf_op jit(solution)/shard_map/ppermute | solution.py:47
  952.9 2.7 shard_map.131.refs_0_
  955.6 67.0 %collective-permute-done.40.part_ref = bf16[16,64,512]{2,1,0:T(8,128)(2,1)} collective-permute-done((bf16[16,64,512]{2,1,0:T(8,128)(2,1)}, bf16[16,64,512]{2,1,0:T(8,128)(2,1)}, u32[]{:S(2)}, u32[]{:S(2)}) %collective-permute-start.40) | collective-permute-done | bytes 1048608 | tf_op jit(solution)/shard_map/ppermute | solution.py:47
  1022.7 2.7 shard_map.132.refs_0_
  1025.4 2.8 shard_map.133
  (189 shorter events, 81.1 us)
Async XLA Ops:
  0.0 54.9 %copy-start.16 = (f32[64]{0:T(128)S(1)}, f32[64]{0:T(128)}, u32[]{:S(2)}) copy-start(f32[64]{0:T(128)} %param.18) | copy-start | bytes 772
  1.0 18.5 %collective-permute-start.20 = (bf16[32,1024]{1,0:T(8,128)(2,1)S(1)}, bf16[32,1024]{1,0:T(8,128)(2,1)S(1)}, u32[]{:S(2)}, u32[]{:S(2)}) collective-permute-start(bf16[32,1024]{1,0:T(8,128)(2,1)S(1)} %constant_dynamic-slice_fusion.2), channel_id=1, source_target_pairs={{0,4},{2,6},{4,0},{6,2},{1,5},{3,7},{5,1},{7,3},{8,12},{10,14},{12... | collective-permute-start | bytes 196616 | tf_op jit(solution)/shard_map/ppermute | solution.py:47
  5.0 14.4 %collective-permute-start.19 = (bf16[32,1024]{1,0:T(8,128)(2,1)S(1)}, bf16[32,1024]{1,0:T(8,128)(2,1)S(1)}, u32[]{:S(2)}, u32[]{:S(2)}) collective-permute-start(bf16[32,1024]{1,0:T(8,128)(2,1)S(1)} %constant_dynamic-slice_fusion.2), channel_id=1, source_target_pairs={{0,2},{2,0},{4,6},{6,4},{1,3},{3,1},{5,7},{7,5},{8,10},{10,8},{12,... | collective-permute-start | bytes 196616 | tf_op jit(solution)/shard_map/ppermute | solution.py:47
  11.6 5.6 collective-permute-start.17
  11.7 5.6 collective-permute-start.16
  13.6 4.1 collective-permute-start.15
  17.3 6.1 collective-permute-start.21
  17.9 7.8 collective-permute-start.18
  24.0 6.4 collective-permute-start.22
  31.3 8.3 collective-permute-start.24
  32.9 6.8 collective-permute-start.23
  32.9 9.5 collective-permute-start.25
  45.8 738.5 %collective-permute-start.26 = (bf16[5,64,64,512]{3,2,1,0:T(8,128)(2,1)}, bf16[5,64,64,512]{3,2,1,0:T(8,128)(2,1)}, u32[]{:S(2)}, u32[]{:S(2)}) collective-permute-start(bf16[5,64,64,512]{3,2,1,0:T(8,128)(2,1)} %refs_4_.5), channel_id=1, source_target_pairs={{0,1},{1,0},{2,3},{3,2},{4,5},{5,4},{6,7},{7,6},{8,9},{9,8},{10,11... | collective-permute-start | bytes 62914568 | tf_op jit(solution)/shard_map/ppermute | solution.py:47
  49.7 101.6 %collective-permute-start.1 = (bf16[16,64,512]{2,1,0:T(8,128)(2,1)}, bf16[16,64,512]{2,1,0:T(8,128)(2,1)S(1)}, u32[]{:S(2)}, u32[]{:S(2)}) collective-permute-start(bf16[16,64,512]{2,1,0:T(8,128)(2,1)} %dynamic-slice_bitcast_fusion.14), channel_id=1, source_target_pairs={{0,4},{2,6},{4,0},{6,2},{1,5},{3,7},{5,1},{7,3},{8,12},{10,14},{12... | collective-permute-start | bytes 3145736 | tf_op jit(solution)/shard_map/ppermute | solution.py:47
  51.4 100.2 %collective-permute-start.2 = (bf16[16,64,512]{2,1,0:T(8,128)(2,1)S(1)}, bf16[16,64,512]{2,1,0:T(8,128)(2,1)S(1)}, u32[]{:S(2)}, u32[]{:S(2)}) collective-permute-start(bf16[16,64,512]{2,1,0:T(8,128)(2,1)S(1)} %get-tuple-element.122), channel_id=1, source_target_pairs={{0,6},{2,4},{4,2},{6,0},{1,7},{3,5},{5,3},{7,1},{8,14},{10,12},{12... | collective-permute-start | bytes 3145736 | tf_op jit(solution)/shard_map/ppermute | solution.py:47
  51.7 104.8 %collective-permute-start = (bf16[16,64,512]{2,1,0:T(8,128)(2,1)S(1)}, bf16[16,64,512]{2,1,0:T(8,128)(2,1)S(1)}, u32[]{:S(2)}, u32[]{:S(2)}) collective-permute-start(bf16[16,64,512]{2,1,0:T(8,128)(2,1)S(1)} %get-tuple-element.123), channel_id=1, source_target_pairs={{0,2},{2,0},{4,6},{6,4},{1,3},{3,1},{5,7},{7,5},{8,10},{10,8},{12,... | collective-permute-start | bytes 3145736 | tf_op jit(solution)/shard_map/ppermute | solution.py:47
  54.9 436.6 %copy-start.13 = (bf16[2,256,256]{2,1,0:T(8,128)(2,1)S(1)}, bf16[2,256,256]{2,1,0:T(8,128)(2,1)}, u32[]{:S(2)}) copy-start(bf16[2,256,256]{2,1,0:T(8,128)(2,1)} %param.15) | copy-start | bytes 786436
  54.9 64.0 %collective-permute-start.8 = (f32[1,64]{1,0:T(1,128)S(1)}, f32[1,64]{1,0:T(1,128)S(1)}, u32[]{:S(2)}, u32[]{:S(2)}) collective-permute-start(f32[1,64]{1,0:T(1,128)S(1)} %bitcast.153), channel_id=1, source_target_pairs={{0,6},{2,4},{4,2},{6,0},{1,7},{3,5},{5,3},{7,1},{8,14},{10,12},{12... | collective-permute-start | bytes 776 | tf_op jit(solution)/shard_map/ppermute | solution.py:47
  119.0 25.8 %collective-permute-start.7 = (f32[1,64]{1,0:T(1,128)S(1)}, f32[1,64]{1,0:T(1,128)S(1)}, u32[]{:S(2)}, u32[]{:S(2)}) collective-permute-start(f32[1,64]{1,0:T(1,128)S(1)} %bitcast.154), channel_id=1, source_target_pairs={{0,4},{2,6},{4,0},{6,2},{1,5},{3,7},{5,1},{7,3},{8,12},{10,14},{12... | collective-permute-start | bytes 776 | tf_op jit(solution)/shard_map/ppermute | solution.py:47
  144.8 3.8 collective-permute-start.6
  148.6 28.1 %collective-permute-start.35 = (bf16[16,64,512]{2,1,0:T(8,128)(2,1)S(1)}, bf16[16,64,512]{2,1,0:T(8,128)(2,1)}, u32[]{:S(2)}, u32[]{:S(2)}) collective-permute-start(bf16[16,64,512]{2,1,0:T(8,128)(2,1)S(1)} %get-tuple-element.116), channel_id=1, source_target_pairs={{0,6},{2,4},{4,2},{6,0},{1,7},{3,5},{5,3},{7,1},{8,14},{10,12},{12... | collective-permute-start | bytes 3145736 | tf_op jit(solution)/shard_map/ppermute | solution.py:47
  151.3 391.4 %copy-start.2 = (bf16[16,64,512]{2,1,0:T(8,128)(2,1)}, bf16[16,64,512]{2,1,0:T(8,128)(2,1)S(1)}, u32[]{:S(2)}) copy-start(bf16[16,64,512]{2,1,0:T(8,128)(2,1)S(1)} %collective-permute-done.1.refs_2_.refs_6_) | copy-start | bytes 3145732
  151.3 135.4 %collective-permute-start.34 = (bf16[16,64,512]{2,1,0:T(8,128)(2,1)S(1)}, bf16[16,64,512]{2,1,0:T(8,128)(2,1)}, u32[]{:S(2)}, u32[]{:S(2)}) collective-permute-start(bf16[16,64,512]{2,1,0:T(8,128)(2,1)S(1)} %get-tuple-element.117), channel_id=1, source_target_pairs={{0,4},{2,6},{4,0},{6,2},{1,5},{3,7},{5,1},{7,3},{8,12},{10,14},{12... | collective-permute-start | bytes 3145736 | tf_op jit(solution)/shard_map/ppermute | solution.py:47
  151.5 391.1 %copy-start.3 = (bf16[16,64,512]{2,1,0:T(8,128)(2,1)}, bf16[16,64,512]{2,1,0:T(8,128)(2,1)S(1)}, u32[]{:S(2)}) copy-start(bf16[16,64,512]{2,1,0:T(8,128)(2,1)S(1)} %collective-permute-done.2.refs_3_.refs_7_) | copy-start | bytes 3145732
  151.6 135.2 %collective-permute-start.33 = (bf16[16,64,512]{2,1,0:T(8,128)(2,1)S(1)}, bf16[16,64,512]{2,1,0:T(8,128)(2,1)}, u32[]{:S(2)}, u32[]{:S(2)}) collective-permute-start(bf16[16,64,512]{2,1,0:T(8,128)(2,1)S(1)} %get-tuple-element.118), channel_id=1, source_target_pairs={{0,2},{2,0},{4,6},{6,4},{1,3},{3,1},{5,7},{7,5},{8,10},{10,8},{12,... | collective-permute-start | bytes 3145736 | tf_op jit(solution)/shard_map/ppermute | solution.py:47
  156.6 390.4 %copy-start.4 = (bf16[16,64,512]{2,1,0:T(8,128)(2,1)}, bf16[16,64,512]{2,1,0:T(8,128)(2,1)S(1)}, u32[]{:S(2)}) copy-start(bf16[16,64,512]{2,1,0:T(8,128)(2,1)S(1)} %collective-permute-done.refs_1_.refs_5_) | copy-start | bytes 3145732
  156.6 132.5 %collective-permute-start.11 = (bf16[16,64,512]{2,1,0:T(8,128)(2,1)S(1)}, bf16[16,64,512]{2,1,0:T(8,128)(2,1)}, u32[]{:S(2)}, u32[]{:S(2)}) collective-permute-start(bf16[16,64,512]{2,1,0:T(8,128)(2,1)S(1)} %get-tuple-element.113), channel_id=1, source_target_pairs={{0,6},{2,4},{4,2},{6,0},{1,7},{3,5},{5,3},{7,1},{8,14},{10,12},{12... | collective-permute-start | bytes 3145736 | tf_op jit(solution)/shard_map/ppermute | solution.py:47
  176.7 199.9 %collective-permute-start.10 = (bf16[16,64,512]{2,1,0:T(8,128)(2,1)}, bf16[16,64,512]{2,1,0:T(8,128)(2,1)}, u32[]{:S(2)}, u32[]{:S(2)}) collective-permute-start(bf16[16,64,512]{2,1,0:T(8,128)(2,1)} %get-tuple-element.114), channel_id=1, source_target_pairs={{0,4},{2,6},{4,0},{6,2},{1,5},{3,7},{5,1},{7,3},{8,12},{10,14},{12... | collective-permute-start | bytes 3145736 | tf_op jit(solution)/shard_map/ppermute | solution.py:47
  286.8 89.9 %collective-permute-start.9 = (bf16[16,64,512]{2,1,0:T(8,128)(2,1)}, bf16[16,64,512]{2,1,0:T(8,128)(2,1)}, u32[]{:S(2)}, u32[]{:S(2)}) collective-permute-start(bf16[16,64,512]{2,1,0:T(8,128)(2,1)} %get-tuple-element.115), channel_id=1, source_target_pairs={{0,2},{2,0},{4,6},{6,4},{1,3},{3,1},{5,7},{7,5},{8,10},{10,8},{12,... | collective-permute-start | bytes 3145736 | tf_op jit(solution)/shard_map/ppermute | solution.py:47
  286.8 90.8 %collective-permute-start.5 = (bf16[16,64,512]{2,1,0:T(8,128)(2,1)}, bf16[16,64,512]{2,1,0:T(8,128)(2,1)S(1)}, u32[]{:S(2)}, u32[]{:S(2)}) collective-permute-start(bf16[16,64,512]{2,1,0:T(8,128)(2,1)} %get-tuple-element.119), channel_id=1, source_target_pairs={{0,6},{2,4},{4,2},{6,0},{1,7},{3,5},{5,3},{7,1},{8,14},{10,12},{12... | collective-permute-start | bytes 3145736 | tf_op jit(solution)/shard_map/ppermute | solution.py:47
  289.0 131.0 %collective-permute-start.4 = (bf16[16,64,512]{2,1,0:T(8,128)(2,1)S(1)}, bf16[16,64,512]{2,1,0:T(8,128)(2,1)}, u32[]{:S(2)}, u32[]{:S(2)}) collective-permute-start(bf16[16,64,512]{2,1,0:T(8,128)(2,1)S(1)} %get-tuple-element.120), channel_id=1, source_target_pairs={{0,4},{2,6},{4,0},{6,2},{1,5},{3,7},{5,1},{7,3},{8,12},{10,14},{12... | collective-permute-start | bytes 3145736 | tf_op jit(solution)/shard_map/ppermute | solution.py:47
  376.6 305.7 %collective-permute-start.29 = (bf16[2,64,64,512]{3,2,1,0:T(8,128)(2,1)}, bf16[2,64,64,512]{3,2,1,0:T(8,128)(2,1)}, u32[]{:S(2)}, u32[]{:S(2)}) collective-permute-start(bf16[2,64,64,512]{3,2,1,0:T(8,128)(2,1)} %slice.25), channel_id=1, source_target_pairs={{0,24},{8,16},{16,8},{24,0},{1,25},{9,17},{17,9},{25,1},{2,26},{10... | collective-permute-start | bytes 25165832 | tf_op jit(solution)/shard_map/ppermute | solution.py:47
  376.6 361.7 %collective-permute-start.28 = (bf16[2,64,64,512]{3,2,1,0:T(8,128)(2,1)}, bf16[2,64,64,512]{3,2,1,0:T(8,128)(2,1)}, u32[]{:S(2)}, u32[]{:S(2)}) collective-permute-start(bf16[2,64,64,512]{3,2,1,0:T(8,128)(2,1)} %slice.25), channel_id=1, source_target_pairs={{0,16},{8,24},{16,0},{24,8},{1,17},{9,25},{17,1},{25,9},{2,18},{10... | collective-permute-start | bytes 25165832 | tf_op jit(solution)/shard_map/ppermute | solution.py:47
  377.5 66.2 %copy-start.11 = (bf16[16,64,512]{2,1,0:T(8,128)(2,1)}, bf16[16,64,512]{2,1,0:T(8,128)(2,1)S(1)}, u32[]{:S(2)}) copy-start(bf16[16,64,512]{2,1,0:T(8,128)(2,1)S(1)} %collective-permute-done.5.refs_3_) | copy-start | bytes 3145732
  377.5 361.3 %collective-permute-start.27 = (bf16[2,64,64,512]{3,2,1,0:T(8,128)(2,1)}, bf16[2,64,64,512]{3,2,1,0:T(8,128)(2,1)}, u32[]{:S(2)}, u32[]{:S(2)}) collective-permute-start(bf16[2,64,64,512]{3,2,1,0:T(8,128)(2,1)} %slice.25), channel_id=1, source_target_pairs={{0,8},{8,0},{16,24},{24,16},{1,9},{9,1},{17,25},{25,17},{2,10},{10... | collective-permute-start | bytes 25165832 | tf_op jit(solution)/shard_map/ppermute | solution.py:47
  420.1 23.7 %collective-permute-start.3 = (bf16[16,64,512]{2,1,0:T(8,128)(2,1)S(1)}, bf16[16,64,512]{2,1,0:T(8,128)(2,1)S(1)}, u32[]{:S(2)}, u32[]{:S(2)}) collective-permute-start(bf16[16,64,512]{2,1,0:T(8,128)(2,1)S(1)} %get-tuple-element.121), channel_id=1, source_target_pairs={{0,2},{2,0},{4,6},{6,4},{1,3},{3,1},{5,7},{7,5},{8,10},{10,8},{12,... | collective-permute-start | bytes 3145736 | tf_op jit(solution)/shard_map/ppermute | solution.py:47
  443.7 25.8 %copy-start.12 = (bf16[16,64,512]{2,1,0:T(8,128)(2,1)}, bf16[16,64,512]{2,1,0:T(8,128)(2,1)S(1)}, u32[]{:S(2)}) copy-start(bf16[16,64,512]{2,1,0:T(8,128)(2,1)S(1)} %collective-permute-done.3.refs_1_) | copy-start | bytes 3145732
  443.7 24.8 %collective-permute-start.14 = (bf16[16,64,512]{2,1,0:T(8,128)(2,1)S(1)}, bf16[16,64,512]{2,1,0:T(8,128)(2,1)S(1)}, u32[]{:S(2)}, u32[]{:S(2)}) collective-permute-start(bf16[16,64,512]{2,1,0:T(8,128)(2,1)S(1)} %get-tuple-element.110), channel_id=1, source_target_pairs={{0,6},{2,4},{4,2},{6,0},{1,7},{3,5},{5,3},{7,1},{8,14},{10,12},{12... | collective-permute-start | bytes 3145736 | tf_op jit(solution)/shard_map/ppermute | solution.py:47
  468.5 1.0 copy-start.10
  469.5 66.4 %collective-permute-start.13 = (bf16[16,64,512]{2,1,0:T(8,128)(2,1)}, bf16[16,64,512]{2,1,0:T(8,128)(2,1)}, u32[]{:S(2)}, u32[]{:S(2)}) collective-permute-start(bf16[16,64,512]{2,1,0:T(8,128)(2,1)} %get-tuple-element.111), channel_id=1, source_target_pairs={{0,4},{2,6},{4,0},{6,2},{1,5},{3,7},{5,1},{7,3},{8,12},{10,14},{12... | collective-permute-start | bytes 3145736 | tf_op jit(solution)/shard_map/ppermute | solution.py:47
  535.9 24.1 %collective-permute-start.12 = (bf16[16,64,512]{2,1,0:T(8,128)(2,1)}, bf16[16,64,512]{2,1,0:T(8,128)(2,1)}, u32[]{:S(2)}, u32[]{:S(2)}) collective-permute-start(bf16[16,64,512]{2,1,0:T(8,128)(2,1)} %get-tuple-element.112), channel_id=1, source_target_pairs={{0,2},{2,0},{4,6},{6,4},{1,3},{3,1},{5,7},{7,5},{8,10},{10,8},{12,... | collective-permute-start | bytes 3145736 | tf_op jit(solution)/shard_map/ppermute | solution.py:47
  547.0 109.5 %copy-start.15 = (f32[64]{0:T(128)S(1)}, f32[64]{0:T(128)}, u32[]{:S(2)}) copy-start(f32[64]{0:T(128)} %param.19) | copy-start | bytes 772
  547.0 110.7 %copy-start.14 = (f32[64,64]{1,0:T(8,128)S(1)}, f32[64,64]{1,0:T(8,128)}, u32[]{:S(2)}) copy-start(f32[64,64]{1,0:T(8,128)} %param.20) | copy-start | bytes 49156
  560.0 25.2 %collective-permute-start.36 = (bf16[16,64,512]{2,1,0:T(8,128)(2,1)}, bf16[16,64,512]{2,1,0:T(8,128)(2,1)}, u32[]{:S(2)}, u32[]{:S(2)}) collective-permute-start(bf16[16,64,512]{2,1,0:T(8,128)(2,1)} %get-tuple-element.87), channel_id=1, source_target_pairs={{0,6},{2,4},{4,2},{6,0},{1,7},{3,5},{5,3},{7,1},{8,14},{10,12},{12... | collective-permute-start | bytes 3145736 | tf_op jit(solution)/shard_map/ppermute | solution.py:47
  585.2 66.0 %collective-permute-start.37 = (bf16[16,64,512]{2,1,0:T(8,128)(2,1)}, bf16[16,64,512]{2,1,0:T(8,128)(2,1)S(1)}, u32[]{:S(2)}, u32[]{:S(2)}) collective-permute-start(bf16[16,64,512]{2,1,0:T(8,128)(2,1)} %get-tuple-element.88), channel_id=1, source_target_pairs={{0,4},{2,6},{4,0},{6,2},{1,5},{3,7},{5,1},{7,3},{8,12},{10,14},{12... | collective-permute-start | bytes 3145736 | tf_op jit(solution)/shard_map/ppermute | solution.py:47
  651.2 16.4 %copy-start.5 = (bf16[16,64,512]{2,1,0:T(8,128)(2,1)}, bf16[16,64,512]{2,1,0:T(8,128)(2,1)S(1)}, u32[]{:S(2)}) copy-start(bf16[16,64,512]{2,1,0:T(8,128)(2,1)S(1)} %collective-permute-done.37.part_ref) | copy-start | bytes 3145732
  651.2 29.3 %collective-permute-start.38 = (bf16[16,64,512]{2,1,0:T(8,128)(2,1)}, bf16[16,64,512]{2,1,0:T(8,128)(2,1)S(1)}, u32[]{:S(2)}, u32[]{:S(2)}) collective-permute-start(bf16[16,64,512]{2,1,0:T(8,128)(2,1)} %get-tuple-element.89), channel_id=1, source_target_pairs={{0,2},{2,0},{4,6},{6,4},{1,3},{3,1},{5,7},{7,5},{8,10},{10,8},{12,... | collective-permute-start | bytes 3145736 | tf_op jit(solution)/shard_map/ppermute | solution.py:47
  680.5 103.8 %copy-start.6 = (bf16[16,64,512]{2,1,0:T(8,128)(2,1)}, bf16[16,64,512]{2,1,0:T(8,128)(2,1)S(1)}, u32[]{:S(2)}) copy-start(bf16[16,64,512]{2,1,0:T(8,128)(2,1)S(1)} %collective-permute-done.38.part_ref) | copy-start | bytes 3145732
  680.5 193.9 %collective-permute-start.45 = (bf16[16,64,512]{2,1,0:T(8,128)(2,1)}, bf16[16,64,512]{2,1,0:T(8,128)(2,1)}, u32[]{:S(2)}, u32[]{:S(2)}) collective-permute-start(bf16[16,64,512]{2,1,0:T(8,128)(2,1)} %get-tuple-element.102), channel_id=1, source_target_pairs={{0,6},{2,4},{4,2},{6,0},{1,7},{3,5},{5,3},{7,1},{8,14},{10,12},{12... | collective-permute-start | bytes 3145736 | tf_op jit(solution)/shard_map/ppermute | solution.py:47
  682.3 194.5 %collective-permute-start.46 = (bf16[16,64,512]{2,1,0:T(8,128)(2,1)}, bf16[16,64,512]{2,1,0:T(8,128)(2,1)}, u32[]{:S(2)}, u32[]{:S(2)}) collective-permute-start(bf16[16,64,512]{2,1,0:T(8,128)(2,1)} %get-tuple-element.103), channel_id=1, source_target_pairs={{0,4},{2,6},{4,0},{6,2},{1,5},{3,7},{5,1},{7,3},{8,12},{10,14},{12... | collective-permute-start | bytes 3145736 | tf_op jit(solution)/shard_map/ppermute | solution.py:47
  738.4 89.4 %collective-permute-start.30 = (bf16[16,64,512]{2,1,0:T(8,128)(2,1)}, bf16[16,64,512]{2,1,0:T(8,128)(2,1)S(1)}, u32[]{:S(2)}, u32[]{:S(2)}) collective-permute-start(bf16[16,64,512]{2,1,0:T(8,128)(2,1)} %get-tuple-element.78), channel_id=1, source_target_pairs={{0,2},{2,0},{4,6},{6,4},{1,3},{3,1},{5,7},{7,5},{8,10},{10,8},{12,... | collective-permute-start | bytes 3145736 | tf_op jit(solution)/shard_map/ppermute | solution.py:47
  738.8 102.4 %collective-permute-start.31 = (bf16[16,64,512]{2,1,0:T(8,128)(2,1)}, bf16[16,64,512]{2,1,0:T(8,128)(2,1)S(1)}, u32[]{:S(2)}, u32[]{:S(2)}) collective-permute-start(bf16[16,64,512]{2,1,0:T(8,128)(2,1)} %get-tuple-element.79), channel_id=1, source_target_pairs={{0,4},{2,6},{4,0},{6,2},{1,5},{3,7},{5,1},{7,3},{8,12},{10,14},{12... | collective-permute-start | bytes 3145736 | tf_op jit(solution)/shard_map/ppermute | solution.py:47
  784.4 62.8 %collective-permute-start.32 = (bf16[16,64,512]{2,1,0:T(8,128)(2,1)}, bf16[16,64,512]{2,1,0:T(8,128)(2,1)S(1)}, u32[]{:S(2)}, u32[]{:S(2)}) collective-permute-start(bf16[16,64,512]{2,1,0:T(8,128)(2,1)} %get-tuple-element.80), channel_id=1, source_target_pairs={{0,6},{2,4},{4,2},{6,0},{1,7},{3,5},{5,3},{7,1},{8,14},{10,12},{12... | collective-permute-start | bytes 3145736 | tf_op jit(solution)/shard_map/ppermute | solution.py:47
  827.8 38.4 %copy-start.7 = (bf16[16,64,512]{2,1,0:T(8,128)(2,1)}, bf16[16,64,512]{2,1,0:T(8,128)(2,1)S(1)}, u32[]{:S(2)}) copy-start(bf16[16,64,512]{2,1,0:T(8,128)(2,1)S(1)} %collective-permute-done.30.part_ref) | copy-start | bytes 3145732
  827.8 49.0 %collective-permute-start.47 = (bf16[16,64,512]{2,1,0:T(8,128)(2,1)}, bf16[16,64,512]{2,1,0:T(8,128)(2,1)}, u32[]{:S(2)}, u32[]{:S(2)}) collective-permute-start(bf16[16,64,512]{2,1,0:T(8,128)(2,1)} %get-tuple-element.104), channel_id=1, source_target_pairs={{0,2},{2,0},{4,6},{6,4},{1,3},{3,1},{5,7},{7,5},{8,10},{10,8},{12,... | collective-permute-start | bytes 3145736 | tf_op jit(solution)/shard_map/ppermute | solution.py:47
  841.2 25.0 %copy-start.8 = (bf16[16,64,512]{2,1,0:T(8,128)(2,1)}, bf16[16,64,512]{2,1,0:T(8,128)(2,1)S(1)}, u32[]{:S(2)}) copy-start(bf16[16,64,512]{2,1,0:T(8,128)(2,1)S(1)} %collective-permute-done.31.part_ref) | copy-start | bytes 3145732
  841.2 57.2 %collective-permute-start.44 = (bf16[16,64,512]{2,1,0:T(8,128)(2,1)}, bf16[16,64,512]{2,1,0:T(8,128)(2,1)}, u32[]{:S(2)}, u32[]{:S(2)}) collective-permute-start(bf16[16,64,512]{2,1,0:T(8,128)(2,1)} %get-tuple-element.97), channel_id=1, source_target_pairs={{0,2},{2,0},{4,6},{6,4},{1,3},{3,1},{5,7},{7,5},{8,10},{10,8},{12,... | collective-permute-start | bytes 3145736 | tf_op jit(solution)/shard_map/ppermute | solution.py:47
  847.2 19.0 %copy-start.9 = (bf16[16,64,512]{2,1,0:T(8,128)(2,1)}, bf16[16,64,512]{2,1,0:T(8,128)(2,1)S(1)}, u32[]{:S(2)}) copy-start(bf16[16,64,512]{2,1,0:T(8,128)(2,1)S(1)} %collective-permute-done.32.part_ref) | copy-start | bytes 3145732
  847.2 85.6 %collective-permute-start.43 = (bf16[16,64,512]{2,1,0:T(8,128)(2,1)}, bf16[16,64,512]{2,1,0:T(8,128)(2,1)}, u32[]{:S(2)}, u32[]{:S(2)}) collective-permute-start(bf16[16,64,512]{2,1,0:T(8,128)(2,1)} %get-tuple-element.96), channel_id=1, source_target_pairs={{0,4},{2,6},{4,0},{6,2},{1,5},{3,7},{5,1},{7,3},{8,12},{10,14},{12... | collective-permute-start | bytes 3145736 | tf_op jit(solution)/shard_map/ppermute | solution.py:47
  874.4 61.1 %collective-permute-start.42 = (bf16[16,64,512]{2,1,0:T(8,128)(2,1)}, bf16[16,64,512]{2,1,0:T(8,128)(2,1)}, u32[]{:S(2)}, u32[]{:S(2)}) collective-permute-start(bf16[16,64,512]{2,1,0:T(8,128)(2,1)} %get-tuple-element.95), channel_id=1, source_target_pairs={{0,6},{2,4},{4,2},{6,0},{1,7},{3,5},{5,3},{7,1},{8,14},{10,12},{12... | collective-permute-start | bytes 3145736 | tf_op jit(solution)/shard_map/ppermute | solution.py:47
  876.8 76.1 %collective-permute-start.41 = (bf16[16,64,512]{2,1,0:T(8,128)(2,1)}, bf16[16,64,512]{2,1,0:T(8,128)(2,1)}, u32[]{:S(2)}, u32[]{:S(2)}) collective-permute-start(bf16[16,64,512]{2,1,0:T(8,128)(2,1)} %get-tuple-element.93), channel_id=1, source_target_pairs={{0,2},{2,0},{4,6},{6,4},{1,3},{3,1},{5,7},{7,5},{8,10},{10,8},{12,... | collective-permute-start | bytes 3145736 | tf_op jit(solution)/shard_map/ppermute | solution.py:47
  876.8 145.9 %collective-permute-start.40 = (bf16[16,64,512]{2,1,0:T(8,128)(2,1)}, bf16[16,64,512]{2,1,0:T(8,128)(2,1)}, u32[]{:S(2)}, u32[]{:S(2)}) collective-permute-start(bf16[16,64,512]{2,1,0:T(8,128)(2,1)} %get-tuple-element.92), channel_id=1, source_target_pairs={{0,4},{2,6},{4,0},{6,2},{1,5},{3,7},{5,1},{7,3},{8,12},{10,14},{12... | collective-permute-start | bytes 3145736 | tf_op jit(solution)/shard_map/ppermute | solution.py:47
  898.4 127.0 %collective-permute-start.39 = (bf16[16,64,512]{2,1,0:T(8,128)(2,1)}, bf16[16,64,512]{2,1,0:T(8,128)(2,1)}, u32[]{:S(2)}, u32[]{:S(2)}) collective-permute-start(bf16[16,64,512]{2,1,0:T(8,128)(2,1)} %get-tuple-element.91), channel_id=1, source_target_pairs={{0,6},{2,4},{4,2},{6,0},{1,7},{3,5},{5,3},{7,1},{8,14},{10,12},{12... | collective-permute-start | bytes 3145736 | tf_op jit(solution)/shard_map/ppermute | solution.py:47
  1025.4 2.8 copy-start.1
  (1 other events, 1.0 us)
where the time goes:
time: 1050 us; the launch traced here: 1030 us
  waiting for transfers between devices  553 us (53%)
  starting transfers between devices  236 us (22%)
  Pallas kernels  173 us (16%)
  local copies, waits for them, and re-layouts  54.6 us (5%)
    ppermute x48, waiting for transfers between devices, send(): return lax.ppermute(array, self.name, pairs)  553 us
    ppermute x48, starting transfers between devices, send(): return lax.ppermute(array, self.name, pairs)  236 us
    pallas_call x20, Pallas kernels, finish(): pl.pallas_call(kernel, grid_spec=pltpu.PrefetchScalarGridSpec(num_scalar_...  54.4 us
    pallas_call x1, Pallas kernels, x_part(): pl.pallas_call(kernel, grid_spec=pltpu.PrefetchScalarGridSpec(num_scalar_...  42.8 us
    pallas_call x1, Pallas kernels, z_part(): pl.pallas_call(kernel, grid=(2, rows // slab), in_specs=[pl.BlockSpec(blo...  42.2 us
    pallas_call x5, Pallas kernels, y_part(): pl.pallas_call(kernel, grid_spec=pltpu.PrefetchScalarGridSpec(num_scalar_...  33.3 us
  transfers between devices with their start and end apart: 48, of which 24 were waited for; matrix products, arithmetic and copies ran while one was open for 6% of the time, Pallas kernels for 17%

commit v1 on v0

--- a/solution.py
+++ b/solution.py
@@ -23,7 +23,7 @@
     ("out", 1),
     ("out", 3),
 )
-IN_FLIGHT = 3
+IN_FLIGHT = 4
 AFTER_REST = 1
 AFTER_FIRST = 3
 Y_TERM = {0: 2, 2: 4, 4: 2}
@@ -389,7 +389,7 @@
             if behind is not None or blocks is not None:
                 source, _ = after((fields, blocks if behind is None else behind))
             blocks = {}
-            for k in step_order(gy.size):
+            for k in step_order(gy.size, (kind, v)):
                 blocks[k] = z_block(source, v, k)
                 if not done and len(blocks) == 1:
                     source, blocks[k] = after((source, blocks[k]))
@@ -399,7 +399,7 @@
             lines = [held[v][k] for k in range(1, gy.size)]
             term_lines = [] if term is None else [held[term][k] for k in range(1, gy.size)]
             whole = y_part(fields, place, v, lines, term, term_lines, matrices, scale_y)
-            going = {k: whole[k] for k in step_order(gy.size)}
+            going = {k: whole[k] for k in step_order(gy.size, (kind, v))}
             if behind is not None:
                 going, _ = after((going, behind))
             if v == AFTER_REST:
@@ -417,8 +417,8 @@
     return total
 
 
-def step_order(size):
-    half = size // 2
+def step_order(size, item):
+    half = size // 2 if item == Y_ITEMS[0] else 1
     return list(range(half, size)) + list(range(1, half))
 
 

time: 1050 us -> 1040 us (level)
  starting transfers between devices: 236 us -> 190 us
  waiting for transfers between devices: 553 us -> 588 us
    ppermute x48, starting transfers between devices: 236 us -> 190 us  [send(): return lax.ppermute(array, self.name, pairs)]
    ppermute x48, waiting for transfers between devices: 553 us -> 588 us  [send(): return lax.ppermute(array, self.name, pairs)]
  transfers between devices with their start and end apart: 48 -> 48, of which waited for: 24 -> 23; matrix products, arithmetic and copies ran while one was open for 6% -> 6% of each run, Pallas kernels for 17% -> 17%
where the time goes in v1:
time: 1040 us; the launch traced here: 1020 us
  waiting for transfers between devices  588 us (57%)
  starting transfers between devices  190 us (18%)
  Pallas kernels  173 us (17%)
  local copies, waits for them, and re-layouts  56.2 us (5%)
    ppermute x48, waiting for transfers between devices, send(): return lax.ppermute(array, self.name, pairs)  588 us
    ppermute x48, starting transfers between devices, send(): return lax.ppermute(array, self.name, pairs)  190 us
    pallas_call x20, Pallas kernels, finish(): pl.pallas_call(kernel, grid_spec=pltpu.PrefetchScalarGridSpec(num_scalar_...  54.5 us
    pallas_call x1, Pallas kernels, x_part(): pl.pallas_call(kernel, grid_spec=pltpu.PrefetchScalarGridSpec(num_scalar_...  42.8 us
    pallas_call x1, Pallas kernels, z_part(): pl.pallas_call(kernel, grid=(2, rows // slab), in_specs=[pl.BlockSpec(blo...  42 us
    pallas_call x5, Pallas kernels, y_part(): pl.pallas_call(kernel, grid_spec=pltpu.PrefetchScalarGridSpec(num_scalar_...  33.4 us
  transfers between devices with their start and end apart: 48, of which 23 were waited for; matrix products, arithmetic and copies ran while one was open for 6% of the time, Pallas kernels for 17%

profile of v1, /device:TPU:0, one launch (start us, length us, event | category | flops | bytes accessed | tf_op | source)
XLA Modules:
  0.0 1020.0 jit_solution(16495344681960032185)
XLA Ops:
  1.0 4.1 collective-permute-start.20
  13.6 2.5 collective-permute-start.15
  19.4 3.9 collective-permute-done.21
  25.9 4.6 collective-permute-done.22
  34.2 5.4 collective-permute-done.24
  39.6 2.7 collective-permute-done.25
  51.8 3.2 collective-permute-start.9
  55.9 63.1 %collective-permute-done.5 = f32[1,64]{1,0:T(1,128)S(1)} collective-permute-done((f32[1,64]{1,0:T(1,128)S(1)}, f32[1,64]{1,0:T(1,128)S(1)}, u32[]{:S(2)}, u32[]{:S(2)}) %collective-permute-start.5) | collective-permute-done | bytes 288 | tf_op jit(solution)/shard_map/ppermute | solution.py:47
  119.0 24.3 %collective-permute-start.4 = (f32[1,64]{1,0:T(1,128)S(1)}, f32[1,64]{1,0:T(1,128)S(1)}, u32[]{:S(2)}, u32[]{:S(2)}) collective-permute-start(f32[1,64]{1,0:T(1,128)S(1)} %bitcast.154), channel_id=1, source_target_pairs={{0,4},{2,6},{4,0},{6,2},{1,5},{3,7},{5,1},{7,3},{8,12},{10,14},{12... | collective-permute-start | bytes 776 | tf_op jit(solution)/shard_map/ppermute | solution.py:47
  146.6 3.1 dynamic-slice_bitcast_fusion.9
  149.7 2.6 collective-permute-start.8
  152.3 3.6 dynamic-slice_bitcast_fusion.6
  157.3 2.6 collective-permute-start.41
  159.9 17.8 %collective-permute-done.8.refs_3_ = bf16[16,64,512]{2,1,0:T(8,128)(2,1)} collective-permute-done((bf16[16,64,512]{2,1,0:T(8,128)(2,1)S(1)}, bf16[16,64,512]{2,1,0:T(8,128)(2,1)}, u32[]{:S(2)}, u32[]{:S(2)}) %collective-permute-start.8) | collective-permute-done | bytes 1048608 | tf_op jit(solution)/shard_map/ppermute | solution.py:47
  177.7 46.6 %collective-permute-start.40 = (bf16[16,64,512]{2,1,0:T(8,128)(2,1)S(1)}, bf16[16,64,512]{2,1,0:T(8,128)(2,1)}, u32[]{:S(2)}, u32[]{:S(2)}) collective-permute-start(bf16[16,64,512]{2,1,0:T(8,128)(2,1)S(1)} %get-tuple-element.117), channel_id=1, source_target_pairs={{0,4},{2,6},{4,0},{6,2},{1,5},{3,7},{5,1},{7,3},{8,12},{10,14},{12... | collective-permute-start | bytes 3145736 | tf_op jit(solution)/shard_map/ppermute | solution.py:47
  224.4 7.9 slice.25
  232.3 55.5 %collective-permute-done.7.refs_2_ = bf16[16,64,512]{2,1,0:T(8,128)(2,1)} collective-permute-done((bf16[16,64,512]{2,1,0:T(8,128)(2,1)}, bf16[16,64,512]{2,1,0:T(8,128)(2,1)}, u32[]{:S(2)}, u32[]{:S(2)}) %collective-permute-start.7) | collective-permute-done | bytes 1048608 | tf_op jit(solution)/shard_map/ppermute | solution.py:47
  289.6 40.9 %collective-permute-done.40.refs_2_.refs_6_ = bf16[16,64,512]{2,1,0:T(8,128)(2,1)} collective-permute-done((bf16[16,64,512]{2,1,0:T(8,128)(2,1)S(1)}, bf16[16,64,512]{2,1,0:T(8,128)(2,1)}, u32[]{:S(2)}, u32[]{:S(2)}) %collective-permute-start.40) | collective-permute-done | bytes 1048608 | tf_op jit(solution)/shard_map/ppermute | solution.py:47
  330.5 3.5 dynamic-slice_bitcast_fusion.3
  334.1 19.6 %collective-permute-done.39.refs_1_.refs_5_ = bf16[16,64,512]{2,1,0:T(8,128)(2,1)} collective-permute-done((bf16[16,64,512]{2,1,0:T(8,128)(2,1)S(1)}, bf16[16,64,512]{2,1,0:T(8,128)(2,1)}, u32[]{:S(2)}, u32[]{:S(2)}) %collective-permute-start.39) | collective-permute-done | bytes 1048608 | tf_op jit(solution)/shard_map/ppermute | solution.py:47
  355.9 21.8 %collective-permute-done.2.refs_3_ = bf16[16,64,512]{2,1,0:T(8,128)(2,1)S(1)} collective-permute-done((bf16[16,64,512]{2,1,0:T(8,128)(2,1)S(1)}, bf16[16,64,512]{2,1,0:T(8,128)(2,1)S(1)}, u32[]{:S(2)}, u32[]{:S(2)}) %collective-permute-start.2) | collective-permute-done | bytes 1048608 | tf_op jit(solution)/shard_map/ppermute | solution.py:47
  378.7 21.9 %collective-permute-start.1 = (bf16[16,64,512]{2,1,0:T(8,128)(2,1)}, bf16[16,64,512]{2,1,0:T(8,128)(2,1)}, u32[]{:S(2)}, u32[]{:S(2)}) collective-permute-start(bf16[16,64,512]{2,1,0:T(8,128)(2,1)} %get-tuple-element.114), channel_id=1, source_target_pairs={{0,4},{2,6},{4,0},{6,2},{1,5},{3,7},{5,1},{7,3},{8,12},{10,14},{12... | collective-permute-start | bytes 3145736 | tf_op jit(solution)/shard_map/ppermute | solution.py:47
  408.0 37.0 %collective-permute-done.1.refs_2_ = bf16[16,64,512]{2,1,0:T(8,128)(2,1)} collective-permute-done((bf16[16,64,512]{2,1,0:T(8,128)(2,1)}, bf16[16,64,512]{2,1,0:T(8,128)(2,1)}, u32[]{:S(2)}, u32[]{:S(2)}) %collective-permute-start.1) | collective-permute-done | bytes 1048608 | tf_op jit(solution)/shard_map/ppermute | solution.py:47
  456.1 7.3 shard_map.110
  463.4 5.8 collective-permute-done.refs_1_
  469.5 22.9 %collective-permute-done.12.part_ref = bf16[16,64,512]{2,1,0:T(8,128)(2,1)S(1)} collective-permute-done((bf16[16,64,512]{2,1,0:T(8,128)(2,1)}, bf16[16,64,512]{2,1,0:T(8,128)(2,1)S(1)}, u32[]{:S(2)}, u32[]{:S(2)}) %collective-permute-start.12) | collective-permute-done | bytes 1048608 | tf_op jit(solution)/shard_map/ppermute | solution.py:47
  497.7 5.2 convert_select_fusion.refs_3_
  502.9 35.2 %collective-permute-done.13.part_ref = bf16[16,64,512]{2,1,0:T(8,128)(2,1)S(1)} collective-permute-done((bf16[16,64,512]{2,1,0:T(8,128)(2,1)}, bf16[16,64,512]{2,1,0:T(8,128)(2,1)S(1)}, u32[]{:S(2)}, u32[]{:S(2)}) %collective-permute-start.13) | collective-permute-done | bytes 1048608 | tf_op jit(solution)/shard_map/ppermute | solution.py:47
  539.6 7.2 shard_map.117
  546.8 7.3 shard_map.116
  554.1 5.6 shard_map.109
  559.7 3.7 dynamic-slice_bitcast_fusion
  566.6 41.4 %collective-permute-start.31 = (bf16[16,64,512]{2,1,0:T(8,128)(2,1)}, bf16[16,64,512]{2,1,0:T(8,128)(2,1)}, u32[]{:S(2)}, u32[]{:S(2)}) collective-permute-start(bf16[16,64,512]{2,1,0:T(8,128)(2,1)} %get-tuple-element.111), channel_id=1, source_target_pairs={{0,4},{2,6},{4,0},{6,2},{1,5},{3,7},{5,1},{7,3},{8,12},{10,14},{12... | collective-permute-start | bytes 3145736 | tf_op jit(solution)/shard_map/ppermute | solution.py:47
  608.0 41.4 %collective-permute-done.28.refs_1_ = bf16[2,64,64,512]{3,2,1,0:T(8,128)(2,1)} collective-permute-done((bf16[2,64,64,512]{3,2,1,0:T(8,128)(2,1)}, bf16[2,64,64,512]{3,2,1,0:T(8,128)(2,1)}, u32[]{:S(2)}, u32[]{:S(2)}) %collective-permute-start.28) | collective-permute-done | bytes 8388640 | tf_op jit(solution)/shard_map/ppermute | solution.py:47
  649.5 2.8 collective-permute-start.45
  652.3 42.0 %z_part.1.refs_4_ = bf16[2,64,64,512]{3,2,1,0:T(8,128)(2,1)} custom-call(bf16[5,64,64,512]{3,2,1,0:T(8,128)(2,1)} %refs_4_.5, bf16[2,64,64,512]{3,2,1,0:T(8,128)(2,1)} %collective-permute-done.27.refs_0_, bf16[2,64,64,512]{3,2,1,0:T(8,128)(2,1)} %collective-permute-done.28.refs_1_, bf16[2,64,64,512]{3,2,1,0:T(8,128)(2,1)} %collective-permute-done.29.refs_2_, ...), custom_call_target="tpu_custom_call" | custom-call | flops 34359738368 | bytes 41943040 | tf_op jit(solution)/shard_map/z_part/pallas_call | solution.py:135
  695.1 42.8 %x_part.1.rest_ref = f32[5,64,64,512]{3,2,1,0:T(8,128)} custom-call(s32[16]{0:T(128)} %add_bitcast_fusion.targets_ref, bf16[5,64,64,512]{3,2,1,0:T(8,128)(2,1)} %refs_4_.5, bf16[5,64,64,512]{3,2,1,0:T(8,128)(2,1)} %collective-permute-done.26.refs_0_, bf16[2,512,512]{2,1,0:T(8,128)(2,1)} %broadcast_select_fusion.refs_1_, f32[1,512]{1,0:T(1,128)} %bitcast.152, ...), custom_call_target="tpu_custom_call" | custom-call | flops 21474836480 | bytes 94371840 | tf_op jit(solution)/shard_map/x_part/pallas_call | solution.py:207
  738.8 2.9 collective-permute-start.42
  741.7 3.5 collective-permute-start.44
  745.2 66.9 %collective-permute-done.46.part_ref = bf16[16,64,512]{2,1,0:T(8,128)(2,1)S(1)} collective-permute-done((bf16[16,64,512]{2,1,0:T(8,128)(2,1)}, bf16[16,64,512]{2,1,0:T(8,128)(2,1)S(1)}, u32[]{:S(2)}, u32[]{:S(2)}) %collective-permute-start.46) | collective-permute-done | bytes 1048608 | tf_op jit(solution)/shard_map/ppermute | solution.py:47
  812.1 6.0 shard_map.111
  818.1 2.7 shard_map.112.refs_0_
  820.8 2.7 shard_map.113.refs_0_
  823.5 2.7 shard_map.114.refs_0_
  826.2 2.7 shard_map.115.refs_0_
  833.0 69.3 %collective-permute-done.43.part_ref = bf16[16,64,512]{2,1,0:T(8,128)(2,1)} collective-permute-done((bf16[16,64,512]{2,1,0:T(8,128)(2,1)}, bf16[16,64,512]{2,1,0:T(8,128)(2,1)}, u32[]{:S(2)}, u32[]{:S(2)}) %collective-permute-start.43) | collective-permute-done | bytes 1048608 | tf_op jit(solution)/shard_map/ppermute | solution.py:47
  906.6 2.7 shard_map.118.refs_0_
  909.3 2.7 shard_map.119.refs_0_
  912.1 2.7 shard_map.120.refs_0_
  914.8 2.7 shard_map.121.refs_0_
  917.5 2.7 shard_map.122.refs_0_
  920.2 2.7 shard_map.123.refs_0_
  922.9 2.7 shard_map.124.refs_0_
  925.6 2.7 shard_map.125.refs_0_
  928.4 2.7 shard_map.126.refs_0_
  931.1 2.7 shard_map.127.refs_0_
  933.8 2.7 shard_map.128.refs_0_
  936.5 2.7 shard_map.129.refs_0_
  939.2 2.7 shard_map.130.refs_0_
  942.0 4.1 collective-permute-done.35.part_ref
  946.1 2.8 shard_map.131.refs_0_
  948.9 65.6 %collective-permute-done.34.part_ref = bf16[16,64,512]{2,1,0:T(8,128)(2,1)} collective-permute-done((bf16[16,64,512]{2,1,0:T(8,128)(2,1)}, bf16[16,64,512]{2,1,0:T(8,128)(2,1)}, u32[]{:S(2)}, u32[]{:S(2)}) %collective-permute-start.34) | collective-permute-done | bytes 1048608 | tf_op jit(solution)/shard_map/ppermute | solution.py:47
  1014.5 2.7 shard_map.132.refs_0_
  1017.2 2.8 shard_map.133
  (187 shorter events, 78.0 us)
Async XLA Ops:
  0.0 1.0 copy-start
  0.0 55.0 %copy-start.15 = (f32[64]{0:T(128)S(1)}, f32[64]{0:T(128)}, u32[]{:S(2)}) copy-start(f32[64]{0:T(128)} %param.18) | copy-start | bytes 772
  1.0 18.5 %collective-permute-start.20 = (bf16[32,1024]{1,0:T(8,128)(2,1)S(1)}, bf16[32,1024]{1,0:T(8,128)(2,1)S(1)}, u32[]{:S(2)}, u32[]{:S(2)}) collective-permute-start(bf16[32,1024]{1,0:T(8,128)(2,1)S(1)} %constant_dynamic-slice_fusion.2), channel_id=1, source_target_pairs={{0,4},{2,6},{4,0},{6,2},{1,5},{3,7},{5,1},{7,3},{8,12},{10,14},{12... | collective-permute-start | bytes 196616 | tf_op jit(solution)/shard_map/ppermute | solution.py:47
  5.0 14.4 %collective-permute-start.19 = (bf16[32,1024]{1,0:T(8,128)(2,1)S(1)}, bf16[32,1024]{1,0:T(8,128)(2,1)S(1)}, u32[]{:S(2)}, u32[]{:S(2)}) collective-permute-start(bf16[32,1024]{1,0:T(8,128)(2,1)S(1)} %constant_dynamic-slice_fusion.2), channel_id=1, source_target_pairs={{0,2},{2,0},{4,6},{6,4},{1,3},{3,1},{5,7},{7,5},{8,10},{10,8},{12,... | collective-permute-start | bytes 196616 | tf_op jit(solution)/shard_map/ppermute | solution.py:47
  11.6 5.6 collective-permute-start.17
  11.7 5.6 collective-permute-start.16
  13.6 4.1 collective-permute-start.15
  17.3 6.1 collective-permute-start.21
  17.9 7.8 collective-permute-start.18
  24.0 6.4 collective-permute-start.22
  31.3 8.3 collective-permute-start.24
  32.9 6.8 collective-permute-start.23
  32.9 9.5 collective-permute-start.25
  45.9 648.4 %collective-permute-start.26 = (bf16[5,64,64,512]{3,2,1,0:T(8,128)(2,1)}, bf16[5,64,64,512]{3,2,1,0:T(8,128)(2,1)}, u32[]{:S(2)}, u32[]{:S(2)}) collective-permute-start(bf16[5,64,64,512]{3,2,1,0:T(8,128)(2,1)} %refs_4_.5), channel_id=1, source_target_pairs={{0,1},{1,0},{2,3},{3,2},{4,5},{5,4},{6,7},{7,6},{8,9},{9,8},{10,11... | collective-permute-start | bytes 62914568 | tf_op jit(solution)/shard_map/ppermute | solution.py:47
  47.4 353.2 %copy-start.12 = (bf16[2,256,256]{2,1,0:T(8,128)(2,1)S(1)}, bf16[2,256,256]{2,1,0:T(8,128)(2,1)}, u32[]{:S(2)}) copy-start(bf16[2,256,256]{2,1,0:T(8,128)(2,1)} %param.15) | copy-start | bytes 786436
  49.7 102.6 %collective-permute-start.10 = (bf16[16,64,512]{2,1,0:T(8,128)(2,1)}, bf16[16,64,512]{2,1,0:T(8,128)(2,1)S(1)}, u32[]{:S(2)}, u32[]{:S(2)}) collective-permute-start(bf16[16,64,512]{2,1,0:T(8,128)(2,1)} %dynamic-slice_bitcast_fusion.14), channel_id=1, source_target_pairs={{0,4},{2,6},{4,0},{6,2},{1,5},{3,7},{5,1},{7,3},{8,12},{10,14},{12... | collective-permute-start | bytes 3145736 | tf_op jit(solution)/shard_map/ppermute | solution.py:47
  51.4 104.5 %collective-permute-start.11 = (bf16[16,64,512]{2,1,0:T(8,128)(2,1)S(1)}, bf16[16,64,512]{2,1,0:T(8,128)(2,1)S(1)}, u32[]{:S(2)}, u32[]{:S(2)}) collective-permute-start(bf16[16,64,512]{2,1,0:T(8,128)(2,1)S(1)} %get-tuple-element.122), channel_id=1, source_target_pairs={{0,6},{2,4},{4,2},{6,0},{1,7},{3,5},{5,3},{7,1},{8,14},{10,12},{12... | collective-permute-start | bytes 3145736 | tf_op jit(solution)/shard_map/ppermute | solution.py:47
  51.8 105.5 %collective-permute-start.9 = (bf16[16,64,512]{2,1,0:T(8,128)(2,1)S(1)}, bf16[16,64,512]{2,1,0:T(8,128)(2,1)S(1)}, u32[]{:S(2)}, u32[]{:S(2)}) collective-permute-start(bf16[16,64,512]{2,1,0:T(8,128)(2,1)S(1)} %get-tuple-element.123), channel_id=1, source_target_pairs={{0,2},{2,0},{4,6},{6,4},{1,3},{3,1},{5,7},{7,5},{8,10},{10,8},{12,... | collective-permute-start | bytes 3145736 | tf_op jit(solution)/shard_map/ppermute | solution.py:47
  55.0 64.0 %collective-permute-start.5 = (f32[1,64]{1,0:T(1,128)S(1)}, f32[1,64]{1,0:T(1,128)S(1)}, u32[]{:S(2)}, u32[]{:S(2)}) collective-permute-start(f32[1,64]{1,0:T(1,128)S(1)} %bitcast.153), channel_id=1, source_target_pairs={{0,6},{2,4},{4,2},{6,0},{1,7},{3,5},{5,3},{7,1},{8,14},{10,12},{12... | collective-permute-start | bytes 776 | tf_op jit(solution)/shard_map/ppermute | solution.py:47
  119.0 25.8 %collective-permute-start.4 = (f32[1,64]{1,0:T(1,128)S(1)}, f32[1,64]{1,0:T(1,128)S(1)}, u32[]{:S(2)}, u32[]{:S(2)}) collective-permute-start(f32[1,64]{1,0:T(1,128)S(1)} %bitcast.154), channel_id=1, source_target_pairs={{0,4},{2,6},{4,0},{6,2},{1,5},{3,7},{5,1},{7,3},{8,12},{10,14},{12... | collective-permute-start | bytes 776 | tf_op jit(solution)/shard_map/ppermute | solution.py:47
  144.8 4.9 collective-permute-start.3
  149.7 28.0 %collective-permute-start.8 = (bf16[16,64,512]{2,1,0:T(8,128)(2,1)S(1)}, bf16[16,64,512]{2,1,0:T(8,128)(2,1)}, u32[]{:S(2)}, u32[]{:S(2)}) collective-permute-start(bf16[16,64,512]{2,1,0:T(8,128)(2,1)S(1)} %get-tuple-element.119), channel_id=1, source_target_pairs={{0,6},{2,4},{4,2},{6,0},{1,7},{3,5},{5,3},{7,1},{8,14},{10,12},{12... | collective-permute-start | bytes 3145736 | tf_op jit(solution)/shard_map/ppermute | solution.py:47
  152.3 303.8 %copy-start.2 = (bf16[16,64,512]{2,1,0:T(8,128)(2,1)}, bf16[16,64,512]{2,1,0:T(8,128)(2,1)S(1)}, u32[]{:S(2)}) copy-start(bf16[16,64,512]{2,1,0:T(8,128)(2,1)S(1)} %collective-permute-done.10.refs_6_.refs_2_) | copy-start | bytes 3145732
  152.3 135.4 %collective-permute-start.7 = (bf16[16,64,512]{2,1,0:T(8,128)(2,1)}, bf16[16,64,512]{2,1,0:T(8,128)(2,1)}, u32[]{:S(2)}, u32[]{:S(2)}) collective-permute-start(bf16[16,64,512]{2,1,0:T(8,128)(2,1)} %get-tuple-element.120), channel_id=1, source_target_pairs={{0,4},{2,6},{4,0},{6,2},{1,5},{3,7},{5,1},{7,3},{8,12},{10,14},{12... | collective-permute-start | bytes 3145736 | tf_op jit(solution)/shard_map/ppermute | solution.py:47
  155.9 300.2 %copy-start.3 = (bf16[16,64,512]{2,1,0:T(8,128)(2,1)}, bf16[16,64,512]{2,1,0:T(8,128)(2,1)S(1)}, u32[]{:S(2)}) copy-start(bf16[16,64,512]{2,1,0:T(8,128)(2,1)S(1)} %collective-permute-done.11.refs_7_.refs_3_) | copy-start | bytes 3145732
  155.9 131.8 %collective-permute-start.6 = (bf16[16,64,512]{2,1,0:T(8,128)(2,1)S(1)}, bf16[16,64,512]{2,1,0:T(8,128)(2,1)}, u32[]{:S(2)}, u32[]{:S(2)}) collective-permute-start(bf16[16,64,512]{2,1,0:T(8,128)(2,1)S(1)} %get-tuple-element.121), channel_id=1, source_target_pairs={{0,2},{2,0},{4,6},{6,4},{1,3},{3,1},{5,7},{7,5},{8,10},{10,8},{12,... | collective-permute-start | bytes 3145736 | tf_op jit(solution)/shard_map/ppermute | solution.py:47
  157.3 298.8 %copy-start.4 = (bf16[16,64,512]{2,1,0:T(8,128)(2,1)}, bf16[16,64,512]{2,1,0:T(8,128)(2,1)S(1)}, u32[]{:S(2)}) copy-start(bf16[16,64,512]{2,1,0:T(8,128)(2,1)S(1)} %collective-permute-done.9.refs_5_.refs_1_) | copy-start | bytes 3145732
  157.3 131.4 %collective-permute-start.41 = (bf16[16,64,512]{2,1,0:T(8,128)(2,1)}, bf16[16,64,512]{2,1,0:T(8,128)(2,1)}, u32[]{:S(2)}, u32[]{:S(2)}) collective-permute-start(bf16[16,64,512]{2,1,0:T(8,128)(2,1)} %get-tuple-element.116), channel_id=1, source_target_pairs={{0,6},{2,4},{4,2},{6,0},{1,7},{3,5},{5,3},{7,1},{8,14},{10,12},{12... | collective-permute-start | bytes 3145736 | tf_op jit(solution)/shard_map/ppermute | solution.py:47
  177.7 152.8 %collective-permute-start.40 = (bf16[16,64,512]{2,1,0:T(8,128)(2,1)S(1)}, bf16[16,64,512]{2,1,0:T(8,128)(2,1)}, u32[]{:S(2)}, u32[]{:S(2)}) collective-permute-start(bf16[16,64,512]{2,1,0:T(8,128)(2,1)S(1)} %get-tuple-element.117), channel_id=1, source_target_pairs={{0,4},{2,6},{4,0},{6,2},{1,5},{3,7},{5,1},{7,3},{8,12},{10,14},{12... | collective-permute-start | bytes 3145736 | tf_op jit(solution)/shard_map/ppermute | solution.py:47
  287.8 278.9 %collective-permute-start.29 = (bf16[2,64,64,512]{3,2,1,0:T(8,128)(2,1)}, bf16[2,64,64,512]{3,2,1,0:T(8,128)(2,1)}, u32[]{:S(2)}, u32[]{:S(2)}) collective-permute-start(bf16[2,64,64,512]{3,2,1,0:T(8,128)(2,1)} %slice.25), channel_id=1, source_target_pairs={{0,24},{8,16},{16,8},{24,0},{1,25},{9,17},{17,9},{25,1},{2,26},{10... | collective-permute-start | bytes 25165832 | tf_op jit(solution)/shard_map/ppermute | solution.py:47
  287.8 361.7 %collective-permute-start.28 = (bf16[2,64,64,512]{3,2,1,0:T(8,128)(2,1)}, bf16[2,64,64,512]{3,2,1,0:T(8,128)(2,1)}, u32[]{:S(2)}, u32[]{:S(2)}) collective-permute-start(bf16[2,64,64,512]{3,2,1,0:T(8,128)(2,1)} %slice.25), channel_id=1, source_target_pairs={{0,16},{8,24},{16,0},{24,8},{1,17},{9,25},{17,1},{25,9},{2,18},{10... | collective-permute-start | bytes 25165832 | tf_op jit(solution)/shard_map/ppermute | solution.py:47
  288.7 360.8 %collective-permute-start.27 = (bf16[2,64,64,512]{3,2,1,0:T(8,128)(2,1)}, bf16[2,64,64,512]{3,2,1,0:T(8,128)(2,1)}, u32[]{:S(2)}, u32[]{:S(2)}) collective-permute-start(bf16[2,64,64,512]{3,2,1,0:T(8,128)(2,1)} %slice.25), channel_id=1, source_target_pairs={{0,8},{8,0},{16,24},{24,16},{1,9},{9,1},{17,25},{25,17},{2,10},{10... | collective-permute-start | bytes 25165832 | tf_op jit(solution)/shard_map/ppermute | solution.py:47
  330.5 23.1 %collective-permute-start.39 = (bf16[16,64,512]{2,1,0:T(8,128)(2,1)S(1)}, bf16[16,64,512]{2,1,0:T(8,128)(2,1)}, u32[]{:S(2)}, u32[]{:S(2)}) collective-permute-start(bf16[16,64,512]{2,1,0:T(8,128)(2,1)S(1)} %get-tuple-element.118), channel_id=1, source_target_pairs={{0,2},{2,0},{4,6},{6,4},{1,3},{3,1},{5,7},{7,5},{8,10},{10,8},{12,... | collective-permute-start | bytes 3145736 | tf_op jit(solution)/shard_map/ppermute | solution.py:47
  353.6 24.0 %collective-permute-start.2 = (bf16[16,64,512]{2,1,0:T(8,128)(2,1)S(1)}, bf16[16,64,512]{2,1,0:T(8,128)(2,1)S(1)}, u32[]{:S(2)}, u32[]{:S(2)}) collective-permute-start(bf16[16,64,512]{2,1,0:T(8,128)(2,1)S(1)} %get-tuple-element.113), channel_id=1, source_target_pairs={{0,6},{2,4},{4,2},{6,0},{1,7},{3,5},{5,3},{7,1},{8,14},{10,12},{12... | collective-permute-start | bytes 3145736 | tf_op jit(solution)/shard_map/ppermute | solution.py:47
  377.7 1.0 copy-start.11
  378.7 66.4 %collective-permute-start.1 = (bf16[16,64,512]{2,1,0:T(8,128)(2,1)}, bf16[16,64,512]{2,1,0:T(8,128)(2,1)}, u32[]{:S(2)}, u32[]{:S(2)}) collective-permute-start(bf16[16,64,512]{2,1,0:T(8,128)(2,1)} %get-tuple-element.114), channel_id=1, source_target_pairs={{0,4},{2,6},{4,0},{6,2},{1,5},{3,7},{5,1},{7,3},{8,12},{10,14},{12... | collective-permute-start | bytes 3145736 | tf_op jit(solution)/shard_map/ppermute | solution.py:47
  445.0 24.1 %collective-permute-start = (bf16[16,64,512]{2,1,0:T(8,128)(2,1)}, bf16[16,64,512]{2,1,0:T(8,128)(2,1)}, u32[]{:S(2)}, u32[]{:S(2)}) collective-permute-start(bf16[16,64,512]{2,1,0:T(8,128)(2,1)} %get-tuple-element.115), channel_id=1, source_target_pairs={{0,2},{2,0},{4,6},{6,4},{1,3},{3,1},{5,7},{7,5},{8,10},{10,8},{12,... | collective-permute-start | bytes 3145736 | tf_op jit(solution)/shard_map/ppermute | solution.py:47
  456.1 37.7 %copy-start.14 = (f32[64]{0:T(128)S(1)}, f32[64]{0:T(128)}, u32[]{:S(2)}) copy-start(f32[64]{0:T(128)} %param.19) | copy-start | bytes 772
  456.1 38.9 %copy-start.13 = (f32[64,64]{1,0:T(8,128)S(1)}, f32[64,64]{1,0:T(8,128)}, u32[]{:S(2)}) copy-start(f32[64,64]{1,0:T(8,128)} %param.20) | copy-start | bytes 49156
  469.2 23.2 %collective-permute-start.12 = (bf16[16,64,512]{2,1,0:T(8,128)(2,1)}, bf16[16,64,512]{2,1,0:T(8,128)(2,1)S(1)}, u32[]{:S(2)}, u32[]{:S(2)}) collective-permute-start(bf16[16,64,512]{2,1,0:T(8,128)(2,1)} %get-tuple-element.68), channel_id=1, source_target_pairs={{0,2},{2,0},{4,6},{6,4},{1,3},{3,1},{5,7},{7,5},{8,10},{10,8},{12,... | collective-permute-start | bytes 3145736 | tf_op jit(solution)/shard_map/ppermute | solution.py:47
  492.3 54.4 %copy-start.5 = (bf16[16,64,512]{2,1,0:T(8,128)(2,1)}, bf16[16,64,512]{2,1,0:T(8,128)(2,1)S(1)}, u32[]{:S(2)}) copy-start(bf16[16,64,512]{2,1,0:T(8,128)(2,1)S(1)} %collective-permute-done.12.part_ref) | copy-start | bytes 3145732
  492.3 45.8 %collective-permute-start.13 = (bf16[16,64,512]{2,1,0:T(8,128)(2,1)}, bf16[16,64,512]{2,1,0:T(8,128)(2,1)S(1)}, u32[]{:S(2)}, u32[]{:S(2)}) collective-permute-start(bf16[16,64,512]{2,1,0:T(8,128)(2,1)} %get-tuple-element.69), channel_id=1, source_target_pairs={{0,4},{2,6},{4,0},{6,2},{1,5},{3,7},{5,1},{7,3},{8,12},{10,14},{12... | collective-permute-start | bytes 3145736 | tf_op jit(solution)/shard_map/ppermute | solution.py:47
  538.1 8.7 copy-start.6
  538.1 26.9 %collective-permute-start.14 = (bf16[16,64,512]{2,1,0:T(8,128)(2,1)}, bf16[16,64,512]{2,1,0:T(8,128)(2,1)S(1)}, u32[]{:S(2)}, u32[]{:S(2)}) collective-permute-start(bf16[16,64,512]{2,1,0:T(8,128)(2,1)} %get-tuple-element.70), channel_id=1, source_target_pairs={{0,6},{2,4},{4,2},{6,0},{1,7},{3,5},{5,3},{7,1},{8,14},{10,12},{12... | collective-permute-start | bytes 3145736 | tf_op jit(solution)/shard_map/ppermute | solution.py:47
  565.0 129.2 %copy-start.7 = (bf16[16,64,512]{2,1,0:T(8,128)(2,1)}, bf16[16,64,512]{2,1,0:T(8,128)(2,1)S(1)}, u32[]{:S(2)}) copy-start(bf16[16,64,512]{2,1,0:T(8,128)(2,1)S(1)} %collective-permute-done.14.part_ref) | copy-start | bytes 3145732
  565.1 172.9 %collective-permute-start.32 = (bf16[16,64,512]{2,1,0:T(8,128)(2,1)}, bf16[16,64,512]{2,1,0:T(8,128)(2,1)}, u32[]{:S(2)}, u32[]{:S(2)}) collective-permute-start(bf16[16,64,512]{2,1,0:T(8,128)(2,1)} %get-tuple-element.110), channel_id=1, source_target_pairs={{0,6},{2,4},{4,2},{6,0},{1,7},{3,5},{5,3},{7,1},{8,14},{10,12},{12... | collective-permute-start | bytes 3145736 | tf_op jit(solution)/shard_map/ppermute | solution.py:47
  566.6 172.1 %collective-permute-start.31 = (bf16[16,64,512]{2,1,0:T(8,128)(2,1)}, bf16[16,64,512]{2,1,0:T(8,128)(2,1)}, u32[]{:S(2)}, u32[]{:S(2)}) collective-permute-start(bf16[16,64,512]{2,1,0:T(8,128)(2,1)} %get-tuple-element.111), channel_id=1, source_target_pairs={{0,4},{2,6},{4,0},{6,2},{1,5},{3,7},{5,1},{7,3},{8,12},{10,14},{12... | collective-permute-start | bytes 3145736 | tf_op jit(solution)/shard_map/ppermute | solution.py:47
  649.5 92.2 %collective-permute-start.30 = (bf16[16,64,512]{2,1,0:T(8,128)(2,1)}, bf16[16,64,512]{2,1,0:T(8,128)(2,1)}, u32[]{:S(2)}, u32[]{:S(2)}) collective-permute-start(bf16[16,64,512]{2,1,0:T(8,128)(2,1)} %get-tuple-element.112), channel_id=1, source_target_pairs={{0,2},{2,0},{4,6},{6,4},{1,3},{3,1},{5,7},{7,5},{8,10},{10,8},{12,... | collective-permute-start | bytes 3145736 | tf_op jit(solution)/shard_map/ppermute | solution.py:47
  649.5 92.2 %collective-permute-start.45 = (bf16[16,64,512]{2,1,0:T(8,128)(2,1)}, bf16[16,64,512]{2,1,0:T(8,128)(2,1)S(1)}, u32[]{:S(2)}, u32[]{:S(2)}) collective-permute-start(bf16[16,64,512]{2,1,0:T(8,128)(2,1)} %get-tuple-element.103), channel_id=1, source_target_pairs={{0,6},{2,4},{4,2},{6,0},{1,7},{3,5},{5,3},{7,1},{8,14},{10,12},{12... | collective-permute-start | bytes 3145736 | tf_op jit(solution)/shard_map/ppermute | solution.py:47
  694.3 117.8 %collective-permute-start.46 = (bf16[16,64,512]{2,1,0:T(8,128)(2,1)}, bf16[16,64,512]{2,1,0:T(8,128)(2,1)S(1)}, u32[]{:S(2)}, u32[]{:S(2)}) collective-permute-start(bf16[16,64,512]{2,1,0:T(8,128)(2,1)} %get-tuple-element.104), channel_id=1, source_target_pairs={{0,4},{2,6},{4,0},{6,2},{1,5},{3,7},{5,1},{7,3},{8,12},{10,14},{12... | collective-permute-start | bytes 3145736 | tf_op jit(solution)/shard_map/ppermute | solution.py:47
  737.9 91.0 %collective-permute-start.47 = (bf16[16,64,512]{2,1,0:T(8,128)(2,1)}, bf16[16,64,512]{2,1,0:T(8,128)(2,1)}, u32[]{:S(2)}, u32[]{:S(2)}) collective-permute-start(bf16[16,64,512]{2,1,0:T(8,128)(2,1)} %get-tuple-element.105), channel_id=1, source_target_pairs={{0,2},{2,0},{4,6},{6,4},{1,3},{3,1},{5,7},{7,5},{8,10},{10,8},{12,... | collective-permute-start | bytes 3145736 | tf_op jit(solution)/shard_map/ppermute | solution.py:47
  738.8 92.3 %collective-permute-start.42 = (bf16[16,64,512]{2,1,0:T(8,128)(2,1)}, bf16[16,64,512]{2,1,0:T(8,128)(2,1)S(1)}, u32[]{:S(2)}, u32[]{:S(2)}) collective-permute-start(bf16[16,64,512]{2,1,0:T(8,128)(2,1)} %get-tuple-element.96), channel_id=1, source_target_pairs={{0,6},{2,4},{4,2},{6,0},{1,7},{3,5},{5,3},{7,1},{8,14},{10,12},{12... | collective-permute-start | bytes 3145736 | tf_op jit(solution)/shard_map/ppermute | solution.py:47
  741.7 160.6 %collective-permute-start.43 = (bf16[16,64,512]{2,1,0:T(8,128)(2,1)}, bf16[16,64,512]{2,1,0:T(8,128)(2,1)}, u32[]{:S(2)}, u32[]{:S(2)}) collective-permute-start(bf16[16,64,512]{2,1,0:T(8,128)(2,1)} %get-tuple-element.97), channel_id=1, source_target_pairs={{0,4},{2,6},{4,0},{6,2},{1,5},{3,7},{5,1},{7,3},{8,12},{10,14},{12... | collective-permute-start | bytes 3145736 | tf_op jit(solution)/shard_map/ppermute | solution.py:47
  741.7 79.1 %copy-start.8 = (bf16[16,64,512]{2,1,0:T(8,128)(2,1)}, bf16[16,64,512]{2,1,0:T(8,128)(2,1)S(1)}, u32[]{:S(2)}) copy-start(bf16[16,64,512]{2,1,0:T(8,128)(2,1)S(1)} %collective-permute-done.45.part_ref) | copy-start | bytes 3145732
  741.7 160.6 %collective-permute-start.44 = (bf16[16,64,512]{2,1,0:T(8,128)(2,1)}, bf16[16,64,512]{2,1,0:T(8,128)(2,1)}, u32[]{:S(2)}, u32[]{:S(2)}) collective-permute-start(bf16[16,64,512]{2,1,0:T(8,128)(2,1)} %get-tuple-element.98), channel_id=1, source_target_pairs={{0,2},{2,0},{4,6},{6,4},{1,3},{3,1},{5,7},{7,5},{8,10},{10,8},{12,... | collective-permute-start | bytes 3145736 | tf_op jit(solution)/shard_map/ppermute | solution.py:47
  812.1 8.7 copy-start.9
  812.1 92.5 %collective-permute-start.38 = (bf16[16,64,512]{2,1,0:T(8,128)(2,1)}, bf16[16,64,512]{2,1,0:T(8,128)(2,1)}, u32[]{:S(2)}, u32[]{:S(2)}) collective-permute-start(bf16[16,64,512]{2,1,0:T(8,128)(2,1)} %get-tuple-element.91), channel_id=1, source_target_pairs={{0,2},{2,0},{4,6},{6,4},{1,3},{3,1},{5,7},{7,5},{8,10},{10,8},{12,... | collective-permute-start | bytes 3145736 | tf_op jit(solution)/shard_map/ppermute | solution.py:47
  829.0 104.8 %collective-permute-start.37 = (bf16[16,64,512]{2,1,0:T(8,128)(2,1)}, bf16[16,64,512]{2,1,0:T(8,128)(2,1)}, u32[]{:S(2)}, u32[]{:S(2)}) collective-permute-start(bf16[16,64,512]{2,1,0:T(8,128)(2,1)} %get-tuple-element.90), channel_id=1, source_target_pairs={{0,4},{2,6},{4,0},{6,2},{1,5},{3,7},{5,1},{7,3},{8,12},{10,14},{12... | collective-permute-start | bytes 3145736 | tf_op jit(solution)/shard_map/ppermute | solution.py:47
  831.1 78.3 %copy-start.10 = (bf16[16,64,512]{2,1,0:T(8,128)(2,1)}, bf16[16,64,512]{2,1,0:T(8,128)(2,1)S(1)}, u32[]{:S(2)}) copy-start(bf16[16,64,512]{2,1,0:T(8,128)(2,1)S(1)} %collective-permute-done.42.part_ref) | copy-start | bytes 3145732
  831.1 105.4 %collective-permute-start.36 = (bf16[16,64,512]{2,1,0:T(8,128)(2,1)}, bf16[16,64,512]{2,1,0:T(8,128)(2,1)}, u32[]{:S(2)}, u32[]{:S(2)}) collective-permute-start(bf16[16,64,512]{2,1,0:T(8,128)(2,1)} %get-tuple-element.89), channel_id=1, source_target_pairs={{0,6},{2,4},{4,2},{6,0},{1,7},{3,5},{5,3},{7,1},{8,14},{10,12},{12... | collective-permute-start | bytes 3145736 | tf_op jit(solution)/shard_map/ppermute | solution.py:47
  902.2 43.8 %collective-permute-start.35 = (bf16[16,64,512]{2,1,0:T(8,128)(2,1)}, bf16[16,64,512]{2,1,0:T(8,128)(2,1)}, u32[]{:S(2)}, u32[]{:S(2)}) collective-permute-start(bf16[16,64,512]{2,1,0:T(8,128)(2,1)} %get-tuple-element.87), channel_id=1, source_target_pairs={{0,2},{2,0},{4,6},{6,4},{1,3},{3,1},{5,7},{7,5},{8,10},{10,8},{12,... | collective-permute-start | bytes 3145736 | tf_op jit(solution)/shard_map/ppermute | solution.py:47
  902.2 112.3 %collective-permute-start.34 = (bf16[16,64,512]{2,1,0:T(8,128)(2,1)}, bf16[16,64,512]{2,1,0:T(8,128)(2,1)}, u32[]{:S(2)}, u32[]{:S(2)}) collective-permute-start(bf16[16,64,512]{2,1,0:T(8,128)(2,1)} %get-tuple-element.86), channel_id=1, source_target_pairs={{0,4},{2,6},{4,0},{6,2},{1,5},{3,7},{5,1},{7,3},{8,12},{10,14},{12... | collective-permute-start | bytes 3145736 | tf_op jit(solution)/shard_map/ppermute | solution.py:47
  904.6 112.6 %collective-permute-start.33 = (bf16[16,64,512]{2,1,0:T(8,128)(2,1)}, bf16[16,64,512]{2,1,0:T(8,128)(2,1)}, u32[]{:S(2)}, u32[]{:S(2)}) collective-permute-start(bf16[16,64,512]{2,1,0:T(8,128)(2,1)} %get-tuple-element.85), channel_id=1, source_target_pairs={{0,6},{2,4},{4,2},{6,0},{1,7},{3,5},{5,3},{7,1},{8,14},{10,12},{12... | collective-permute-start | bytes 3145736 | tf_op jit(solution)/shard_map/ppermute | solution.py:47
  1017.2 2.8 copy-start.1
